TPU v7x, 1024 devices: a whole 8x8x8 slice. The times are simulated.
1024 devices in a mesh: expert: 64 (over z, y), dp: 16 (over x, core).
Axes of the slice: x: 8, y: 8, z: 8, core: 2. Of those that a mesh axis runs over, the one named last changes fastest.
Arguments:
- cotangent: bfloat16 [131072, 2048], P(('expert', 'dp')), may hold values from -4 to 4
- router_probs: bfloat16 [131072, 1], P(('expert', 'dp')), may hold values from 0.049804688 to 0.59765625
- slot_ids: int32 [131072, 1], P(('expert', 'dp')), may hold values from 0 to 63; in each aligned block of 128 rows (0 to 127, 128 to 255, ...) at most 3 rows name the same one
- saved_hidden: bfloat16 [64, 3072, 1024], P('expert', 'dp'), may hold values from -6 to 6
- down_weight: bfloat16 [64, 2048, 512], P('expert', 'dp'), as said below
Outputs:
- grad_down: float32 [64, 2048, 512], P('expert', 'dp')
- grad_hidden: bfloat16 [64, 3072, 1024], P('expert', 'dp')
- grad_probs: float32 [131072, 1], P(('expert', 'dp'))
Inputs may be any that keep to these rules, and one draw needn't show every extreme that they name: `slot_ids`: in the 128 tokens of one device, each token names one slot, no slot is named by more than 3 tokens, a bound that some block reaches. `down_weight`: slots s and s + 32 hold the same expert's weights.
All inputs are finite; a program needn't handle non-finite values.
Results may differ from a plain program's by a relative error of at most 0.007.
Values may be sent and summed in bfloat16 or wider, within the bound.
No kernel may reach another device: no remote copies, remote signals or barrier semaphores. Data moves between devices by JAX's collectives and lax.ppermute only.
A program may use at most 32 MiB of HBM per device.

v0:
```python
import math

import jax
import jax.numpy as jnp
from jax import lax
from jax.sharding import PartitionSpec as P


def side_by_side(arrays, axis, split_dim, concat_dim, along):
    widths = [math.prod(a.shape[along:]) for a in arrays]
    both = jnp.concatenate(
        [a.reshape(*a.shape[:along], w) for a, w in zip(arrays, widths)], axis=along
    )
    filled = lax.all_to_all(both, axis, split_axis=split_dim, concat_axis=concat_dim, tiled=True)
    tiles = jnp.split(filled, [sum(widths[:k]) for k in range(1, len(widths))], axis=along)
    return tuple(
        (b.reshape(*filled.shape[:along], *a.shape[along:]) for a, b in zip(arrays, tiles))
    )


def from_partner(block, axis, bit):
    count = lax.axis_size(axis)
    route = []
    for low in range(count):
        high = low | 1 << bit
        if high != low and high < count:
            route += [(low, high), (high, low)]
    return lax.ppermute(block, axis, route)


def on_device(cotangent, router_probs, slot_ids, saved_hidden, down_weight):
    expert_count = lax.axis_size("expert")
    tok_count, pick_count = slot_ids.shape
    model_width = cotangent.shape[1]
    capacity = 3 * tok_count * pick_count // (2 * expert_count)
    flat_slot = slot_ids.reshape(-1)
    slot_hits = (flat_slot[:, None] == jnp.arange(expert_count, dtype=jnp.int32)[None, :]).astype(
        jnp.int32
    )
    earlier = jnp.cumsum(slot_hits, axis=0) - slot_hits
    position = jnp.sum(earlier * slot_hits, axis=1)
    target = flat_slot * capacity + position
    places = (
        target[:, None] == jnp.arange(expert_count * capacity, dtype=jnp.int32)[None, :]
    ).astype(jnp.float32)
    places = places.reshape(tok_count, pick_count, expert_count * capacity)
    spread = jnp.sum(places, axis=1).astype(jnp.bfloat16)
    sent_rows = lax.dot_general(
        spread, cotangent, (((0,), (0,)), ((), ())), preferred_element_type=jnp.float32
    ).astype(jnp.bfloat16)
    sent_probs = jnp.einsum("tkr,tk->r", places, router_probs.astype(jnp.float32)).astype(
        jnp.bfloat16
    )
    rows_in, probs_in = side_by_side(
        (
            sent_rows.reshape(expert_count, capacity, model_width),
            sent_probs.reshape(expert_count, capacity),
        ),
        "expert",
        0,
        1,
        2,
    )
    cot_rows = rows_in[0]
    prob_rows = probs_in[0]
    hidden = saved_hidden[0]
    hidden_width = hidden.shape[1] // 2
    gate_pre = hidden[:, :hidden_width].astype(jnp.float32)
    up_pre = hidden[:, hidden_width:].astype(jnp.float32)
    gate_sig = jax.nn.sigmoid(gate_pre)
    gate_act = gate_pre * gate_sig
    activation = (gate_act * up_pre).astype(jnp.bfloat16)
    scaled = (prob_rows.astype(jnp.float32)[:, None] * cot_rows.astype(jnp.float32)).astype(
        jnp.bfloat16
    )
    weight_piece = lax.all_gather(down_weight, "dp", axis=1, tiled=True)[0]
    out_part = lax.dot_general(
        activation, weight_piece, (((1,), (1,)), ((), ())), preferred_element_type=jnp.float32
    )
    cot_part = cot_rows.astype(jnp.float32)
    prob_grad = jnp.sum(cot_part * out_part, axis=1)
    grad_act = jnp.dot(scaled, weight_piece, preferred_element_type=jnp.float32)
    grad_act, prob_grad = (grad_act, prob_grad)
    grad_gate = grad_act * up_pre * gate_sig * (1.0 + gate_pre * (1.0 - gate_sig))
    grad_up = grad_act * gate_act
    grad_hidden = jnp.concatenate([grad_gate, grad_up], axis=1).astype(jnp.bfloat16)[None]
    prob_back = lax.all_to_all(
        prob_grad[None, :], "expert", split_axis=1, concat_axis=0, tiled=True
    )
    grad_probs = jnp.einsum("tkr,r->tk", places, prob_back.reshape(-1))
    weight_grad = lax.psum_scatter(
        lax.dot_general(
            scaled, activation, (((0,), (0,)), ((), ())), preferred_element_type=jnp.float32
        ),
        "dp",
        scatter_dimension=0,
        tiled=True,
    )
    partner = from_partner(
        weight_grad.astype(jnp.bfloat16), "expert", expert_count.bit_length() - 2
    ).astype(weight_grad.dtype)
    grad_down = (weight_grad + partner)[None]
    return (grad_down, grad_hidden, grad_probs)


def solution(mesh):
    placed = (
        P(("expert", "dp"), None),
        P(("expert", "dp"), None),
        P(("expert", "dp"), None),
        P("expert", "dp", None),
        P("expert", "dp", None),
    )
    return jax.shard_map(
        on_device,
        mesh=mesh,
        in_specs=placed,
        out_specs=(P("expert", "dp", None), P("expert", "dp", None), P(("expert", "dp"), None)),
        check_vma=False,
    )
```

profile of v0, /device:TPU:32, one launch (start us, length us, event | category | flops | bytes accessed | tf_op | source)
XLA Modules:
  0.0 159.7 jit_solution(3485619348358177693)
XLA Ops:
  7.2 0.0 copy-start
  7.2 0.0 all-gather.2.cloned.1.call-start
  7.2 0.7 all-gather.2.cloned.1.call-update
  7.9 0.0 reduce-scatter.2.cloned.1.call-start
  8.0 0.7 fusion.32
  8.7 0.2 reduce_window_sum.11
  8.9 0.8 select_reduce_fusion
  9.7 0.7 fusion.35
  10.4 0.8 fusion.29
  11.2 0.3 reshape_reshape.4
  11.4 0.0 copy-done
  11.5 0.5 convolution_convert_fusion
  11.9 0.5 reshape.146
  12.4 0.6 pad_maximum_fusion
  13.0 0.0 copy-start.1
  13.0 53.5 %all_to_all.25 = bf16[64,3,2049]{2,1,0:T(4,128)(2,1)S(1)} all-to-all(bf16[64,3,2049]{2,1,0:T(4,128)(2,1)S(1)} %pad_maximum_fusion), channel_id=1, replica_groups=mesh['expert'=64,'dp'=16] {'expert'}, dimensions={0} | all-to-all | bytes 1573632 | tf_op jit(solution)/shard_map/all_to_all | solution.py:14
  66.5 0.7 all_to_all.20
  67.3 0.1 convert_reduce_fusion
  67.4 0.0 copy-done.1
  67.4 2.8 %fusion.11 = f32[2048,512]{1,0:T(8,128)} fusion(f32[192]{0:T(256)S(1)} %convert_reduce_fusion, bf16[1,192,2049]{2,1,0:T(8,128)(2,1)S(1)} %all_to_all.20, bf16[192,1024]{1,0:T(8,128)(2,1)S(1)} %bitcast.53), kind=kOutput, calls=%fused_computation.14 | convolution fusion | flops 404619264 | bytes 5374976 | tf_op jit(solution)/shard_map/dot_general | solution.py:92
  70.2 0.0 reduce-scatter.2.cloned.1.call-update
  70.2 0.0 all-gather.2.cloned.1.call-done
  70.2 2.5 %fusion.6 = f32[192]{0:T(256)S(1)} fusion(bf16[1,2048,512]{2,1,0:T(8,128)(2,1)} %all-gather.2.cloned.1.call-done, bf16[1,192,2049]{2,1,0:T(8,128)(2,1)S(1)} %all_to_all.20, bf16[192,1024]{1,0:T(8,128)(2,1)S(1)} %bitcast.54), kind=kOutput, calls=%fused_computation.10 | convolution fusion | flops 404619072 | bytes 3277568 | tf_op jit(solution)/shard_map/dot_general | solution.py:77
  72.8 0.8 all_to_all.21
  73.6 9.8 %all-to-all-start.1 = ((f32[1,64,3]{2,0,1:T(1,128)}), f32[1,64,3]{2,0,1:T(1,128)S(1)}, u32[]{:S(2)}, u32[]{:S(2)}) async-start(f32[1,64,3]{2,0,1:T(1,128)} %bitcast.13), calls=%async_computation.2 | async-start | bytes 65536 | tf_op jit(solution)/shard_map/all_to_all | solution.py:87
  83.4 2.3 %fusion.26 = (bf16[1,192,512]{2,1,0:T(8,128)(2,1)S(1)}, bf16[1,192,512]{2,1,0:T(8,128)(2,1)S(1)}) fusion(bf16[192,1024]{1,0:T(8,128)(2,1)S(1)} %bitcast.55, bf16[1,2048,512]{2,1,0:T(8,128)(2,1)} %all-gather.2.cloned.1.call-done, f32[192]{0:T(256)S(1)} %convert_reduce_fusion, bf16[1,192,2049]{2,1,0:T(8,128)(2,1)S(1)} %all_to_all.20), kind=kOutput, calls=%fused_computation.36 | convolution fusion | flops 405307392 | bytes 3671040 | tf_op jit(solution)/shard_map/dot_general | solution.py:82
  85.7 0.8 pad_maximum_fusion.1
  86.5 7.0 %all-to-all-done.1 = f32[1,64,3]{2,0,1:T(1,128)S(1)} async-done(((f32[1,64,3]{2,0,1:T(1,128)}), f32[1,64,3]{2,0,1:T(1,128)S(1)}, u32[]{:S(2)}, u32[]{:S(2)}) %all-to-all-start.1) | async-done | bytes 800 | tf_op jit(solution)/shard_map/all_to_all | solution.py:87
  93.5 0.5 broadcast.54
  94.0 0.7 reduce.5
  94.7 0.1 reshape.153
  94.9 42.5 %reduce-scatter.2.cloned.1.call-done = f32[128,512]{1,0:T(8,128)} async-done(((f32[2048,512]{1,0:T(8,128)}), f32[128,512]{1,0:T(8,128)}) %reduce-scatter.2.cloned.1.call-update) | async-done | bytes 262160 | tf_op jit(solution)/shard_map/reduce_scatter | solution.py:91
  137.4 1.0 convert_element_type.82
  138.4 8.7 %collective-permute-start = (bf16[128,512]{1,0:T(8,128)(2,1)S(1)}, bf16[128,512]{1,0:T(8,128)(2,1)S(1)}, u32[]{:S(2)}, u32[]{:S(2)}) collective-permute-start(bf16[128,512]{1,0:T(8,128)(2,1)S(1)} %convert_element_type.82), channel_id=1, source_target_pairs={{0,512},{512,0},{16,528},{528,16},{32,544},{544,32},{48,560},{560,... | collective-permute-start | bytes 393224 | tf_op jit(solution)/shard_map/ppermute | solution.py:28
  147.1 0.7 convolution_bitcast_fusion
  147.8 3.4 %collective-permute-done = bf16[128,512]{1,0:T(8,128)(2,1)S(1)} collective-permute-done((bf16[128,512]{1,0:T(8,128)(2,1)S(1)}, bf16[128,512]{1,0:T(8,128)(2,1)S(1)}, u32[]{:S(2)}, u32[]{:S(2)}) %collective-permute-start) | collective-permute-done | bytes 131104 | tf_op jit(solution)/shard_map/ppermute | solution.py:28
  151.2 1.7 %add_bitcast_fusion = f32[1,128,512]{2,1,0:T(8,128)} fusion(f32[128,512]{1,0:T(8,128)} %reduce-scatter.2.cloned.1.call-done, bf16[128,512]{1,0:T(8,128)(2,1)S(1)} %collective-permute-done), kind=kLoop, calls=%fused_computation.34 | loop fusion | flops 131072 | bytes 655360 | tf_op jit(solution)/shard_map/broadcast_in_dim | solution.py:102
  (1 shorter events, 0.0 us)
Async XLA Ops:
  7.2 4.3 %copy-start = (bf16[128,2048]{1,0:T(8,128)(2,1)S(1)}, bf16[128,2048]{1,0:T(8,128)(2,1)}, u32[]{:S(2)}) copy-start(bf16[128,2048]{1,0:T(8,128)(2,1)} %param.5) | copy-start | bytes 1572868
  7.2 63.1 %all-gather.2.cloned.1.call-start = ((), (), s32[]{:S(2)}) async-start(), calls=%async_computation.4 | async-start | bytes 2228224 | tf_op jit(solution)/shard_map/all_gather | solution.py:76
  7.9 129.5 %reduce-scatter.2.cloned.1.call-start = ((), (), s32[]{:S(2)}) async-start(), calls=%async_computation.3 | async-start | bytes 4456448 | tf_op jit(solution)/shard_map/reduce_scatter | solution.py:91
  13.0 54.4 %copy-start.1 = (bf16[1,192,1024]{2,1,0:T(8,128)(2,1)S(1)}, bf16[1,192,1024]{2,1,0:T(8,128)(2,1)}, u32[]{:S(2)}) copy-start(bf16[1,192,1024]{2,1,0:T(8,128)(2,1)} %param.8) | copy-start | bytes 1179652
  73.6 19.9 %all-to-all-start.1 = ((f32[1,64,3]{2,0,1:T(1,128)}), f32[1,64,3]{2,0,1:T(1,128)S(1)}, u32[]{:S(2)}, u32[]{:S(2)}) async-start(f32[1,64,3]{2,0,1:T(1,128)} %bitcast.13), calls=%async_computation.2 | async-start | bytes 65536 | tf_op jit(solution)/shard_map/all_to_all | solution.py:87
  138.4 12.8 %collective-permute-start = (bf16[128,512]{1,0:T(8,128)(2,1)S(1)}, bf16[128,512]{1,0:T(8,128)(2,1)S(1)}, u32[]{:S(2)}, u32[]{:S(2)}) collective-permute-start(bf16[128,512]{1,0:T(8,128)(2,1)S(1)} %convert_element_type.82), channel_id=1, source_target_pairs={{0,512},{512,0},{16,528},{528,16},{32,544},{544,32},{48,560},{560,... | collective-permute-start | bytes 393224 | tf_op jit(solution)/shard_map/ppermute | solution.py:28
Sparse Core Ops, SparseCore 0:
  10.7 55.1 all-gather.1
  70.3 67.0 reduce-scatter.1
where the time goes:
time: 160 us
  waiting for transfers between devices  53.6 us (34%)
  blocking collectives  53.5 us (33%)
  starting transfers between devices  18.6 us (12%)
  between operations  14.2 us (9%)
  matrix products  9.6 us (6%)
  other arithmetic  7.26 us (5%)
  local copies, waits for them, and re-layouts  2.94 us (2%)
    all_to_all x1, blocking collectives, side_by_side(): lax.all_to_all(both, axis, split_axis=split_dim, concat_axis=concat_dim,...  53.5 us
    reduce_scatter x1, waiting for transfers between devices, on_device(): lax.psum_scatter(lax.dot_general(scaled, activation, (((0,), (0,)), ((),...  42.5 us
    all_to_all x1, starting transfers between devices, on_device(): lax.all_to_all(prob_grad[None, :], 'expert', split_axis=1, concat_axis=0,...  9.82 us
    ppermute x1, starting transfers between devices, from_partner(): return lax.ppermute(block, axis, route)  8.73 us
    all_to_all x1, waiting for transfers between devices, on_device(): lax.all_to_all(prob_grad[None, :], 'expert', split_axis=1, concat_axis=0,...  6.98 us
    ppermute x1, waiting for transfers between devices, from_partner(): return lax.ppermute(block, axis, route)  3.44 us
  transfers between devices with their start and end apart: 4, of which 3 were waited for; matrix products, arithmetic and copies ran while one was open for 10% of the time, Pallas kernels for 0%

commit v1 on v0

v1 whole, which is shorter than its diff:
```python
import jax
import jax.numpy as jnp
from jax import lax
from jax.sharding import Mesh, PartitionSpec as P


BF = jnp.bfloat16
F32 = jnp.float32
SPREAD = ("core", "expert")


def swap(block, axis, bit):
    count = lax.axis_size(axis)
    return lax.ppermute(block, axis, [(k, k ^ bit) for k in range(count)])


def shift(block, axis, step):
    count = lax.axis_size(axis)
    return lax.ppermute(block, axis, [(k, (k + step) % count) for k in range(count)])


def exchange(blocks, axis):
    return lax.all_to_all(blocks, axis, split_axis=0, concat_axis=0, tiled=True)


def swiglu(hidden):
    ff = hidden.shape[1] // 2
    gate = hidden[:, :ff].astype(F32)
    up = hidden[:, ff:].astype(F32)
    sig = jax.nn.sigmoid(gate)
    silu = gate * sig
    return gate, up, sig, silu, (silu * up).astype(BF)


def on_device(cotangent, router_probs, slot_ids, saved_hidden, down_weight):
    slots = lax.axis_size("expert")
    chips = lax.axis_size("x")
    core = lax.axis_index("core")
    tokens, width = cotangent.shape
    cap = saved_hidden.shape[1] // slots
    lanes = width // (2 * chips)
    rows = slots * cap
    first = core == 0
    hidden = saved_hidden[0]
    ff = hidden.shape[1] // 2

    ids = slot_ids.reshape(-1)
    same = (ids[:, None] == ids[None, :]) & (
        jnp.arange(tokens)[None, :] < jnp.arange(tokens)[:, None]
    )
    position = jnp.sum(same.astype(jnp.int32), axis=1)
    target = ids * cap + position
    place = target[:, None] == jnp.arange(rows, dtype=jnp.int32)[None, :]
    probs = router_probs.astype(F32)
    spread = jnp.where(place, probs, 0.0).astype(BF)
    sent = lax.dot_general(
        spread, cotangent, (((0,), (0,)), ((), ())), preferred_element_type=F32
    ).astype(BF)
    sent = sent.reshape(slots, cap, chips, 2, lanes).transpose(3, 0, 1, 2, 4)
    sent = sent.reshape(2 * slots, cap * chips, lanes)
    got = exchange(sent, SPREAD)
    scaled = got.reshape(2 * rows, chips * lanes)

    chip = lax.axis_index("x")
    weight = jnp.zeros((chips,) + down_weight.shape[1:], BF)
    weight = lax.dynamic_update_index_in_dim(weight, down_weight[0], chip, 0)
    for step in range(1, chips):
        block = shift(down_weight[0], "x", step)
        weight = lax.dynamic_update_index_in_dim(
            weight, block, jnp.bitwise_and(chip - step, chips - 1), 0
        )
    weight = weight.reshape(chips * lanes, ff)

    activation = swiglu(hidden)[-1]
    other_activation = swap(activation, "core", 1)
    both = jnp.concatenate(
        [
            jnp.where(first, activation, other_activation),
            jnp.where(first, other_activation, activation),
        ],
        axis=0,
    )

    partial = lax.dot_general(
        scaled, both, (((0,), (0,)), ((), ())), preferred_element_type=F32
    ).astype(BF)
    parts = exchange(partial.reshape(chips, lanes, ff), "x")
    slot_grad = jnp.sum(parts.astype(F32), axis=0)
    rounded = slot_grad.astype(BF)
    partner = swap(rounded, "expert", slots // 2)
    grad_down = (slot_grad + partner.astype(F32))[None]

    half = jnp.dot(scaled, weight, preferred_element_type=F32)
    low, high = half[:rows], half[rows:]
    mine = jnp.where(first, low, high)
    theirs = jnp.where(first, high, low)
    theirs = swap(theirs, "core", 1)
    hidden, theirs = lax.optimization_barrier((hidden, theirs))
    gate, up, sig, silu, activation = swiglu(hidden)
    grad_act = mine + theirs
    grad_gate = grad_act * up * sig * (1.0 + gate * (1.0 - sig))
    grad_up = grad_act * silu
    grad_hidden = jnp.concatenate([grad_gate, grad_up], axis=1).astype(BF)[None]
    weighted = jnp.sum(grad_act * activation.astype(F32), axis=1)
    back = exchange(weighted.reshape(slots, cap), "expert").reshape(rows)
    grad_probs = (
        jnp.sum(jnp.where(place, back[None, :], 0.0), axis=1, keepdims=True) / probs
    )
    return (grad_down, grad_hidden, grad_probs)


def solution(mesh):
    slots, groups = mesh.shape["expert"], mesh.shape["dp"]
    fine = Mesh(mesh.devices.reshape(slots, groups // 2, 2), ("expert", "x", "core"))
    dp = ("x", "core")
    tok = P(("expert", "x", "core"), None)
    slot = P("expert", dp, None)

    return jax.shard_map(
        on_device,
        mesh=fine,
        in_specs=(tok, tok, tok, slot, slot),
        out_specs=(slot, slot, tok),
        check_vma=False,
    )
```

time: 160 us -> 147 us (0.919)
  the two profiles are of different devices: /device:TPU:32 before, /device:TPU:1 now
where the time goes in v1:
time: 147 us; the launch traced here: 146 us
  starting transfers between devices  73.8 us (50%)
  waiting for transfers between devices  57.4 us (39%)
  other arithmetic  7.04 us (5%)
  local copies, waits for them, and re-layouts  3.52 us (2%)
  matrix products  3.27 us (2%)
    all_to_all x3, waiting for transfers between devices, exchange(): return lax.all_to_all(blocks, axis, split_axis=0, concat_axis=0, tiled=True)  47.3 us
    all_to_all x3, starting transfers between devices, exchange(): return lax.all_to_all(blocks, axis, split_axis=0, concat_axis=0, tiled=True)  36.2 us
    ppermute x7, starting transfers between devices, shift(): lax.ppermute(block, axis, [(k, (k + step) % count) for k in range(count)])  29 us
    ppermute x3, starting transfers between devices, swap(): return lax.ppermute(block, axis, [(k, k ^ bit) for k in range(count)])  8.47 us
    ppermute x3, waiting for transfers between devices, swap(): return lax.ppermute(block, axis, [(k, k ^ bit) for k in range(count)])  8.27 us
  transfers between devices with their start and end apart: 13, of which 6 were waited for; matrix products, arithmetic and copies ran while one was open for 8% of the time, Pallas kernels for 0%

profile of v1, /device:TPU:1, one launch (start us, length us, event | category | flops | bytes accessed | tf_op | source)
XLA Modules:
  0.0 145.9 jit_solution(11889571427721809242)
XLA Ops:
  0.6 0.0 copy-start
  0.6 4.1 %collective-permute-start.2 = (bf16[128,512]{1,0:T(8,128)(2,1)}, bf16[128,512]{1,0:T(8,128)(2,1)S(1)}, u32[]{:S(2)}, u32[]{:S(2)}) collective-permute-start(bf16[128,512]{1,0:T(8,128)(2,1)} %bitcast.50), channel_id=1, source_target_pairs={{0,2},{2,4},{4,6},{6,8},{8,10},{10,12},{12,14},{14,0},{1,3},{3,5},... | collective-permute-start | bytes 393224 | tf_op jit(solution)/shard_map/ppermute | solution.py:19
  4.7 4.0 %collective-permute-start.3 = (bf16[128,512]{1,0:T(8,128)(2,1)}, bf16[128,512]{1,0:T(8,128)(2,1)S(1)}, u32[]{:S(2)}, u32[]{:S(2)}) collective-permute-start(bf16[128,512]{1,0:T(8,128)(2,1)} %bitcast.51), channel_id=1, source_target_pairs={{0,4},{2,6},{4,8},{6,10},{8,12},{10,14},{12,0},{14,2},{1,5},{3,7},... | collective-permute-start | bytes 393224 | tf_op jit(solution)/shard_map/ppermute | solution.py:19
  8.8 4.4 %collective-permute-start.4 = (bf16[128,512]{1,0:T(8,128)(2,1)}, bf16[128,512]{1,0:T(8,128)(2,1)S(1)}, u32[]{:S(2)}, u32[]{:S(2)}) collective-permute-start(bf16[128,512]{1,0:T(8,128)(2,1)} %bitcast.52), channel_id=1, source_target_pairs={{0,6},{2,8},{4,10},{6,12},{8,14},{10,0},{12,2},{14,4},{1,7},{3,9},... | collective-permute-start | bytes 393224 | tf_op jit(solution)/shard_map/ppermute | solution.py:19
  13.2 3.9 %collective-permute-start.5 = (bf16[128,512]{1,0:T(8,128)(2,1)}, bf16[128,512]{1,0:T(8,128)(2,1)S(1)}, u32[]{:S(2)}, u32[]{:S(2)}) collective-permute-start(bf16[128,512]{1,0:T(8,128)(2,1)} %bitcast.53), channel_id=1, source_target_pairs={{0,8},{2,10},{4,12},{6,14},{8,0},{10,2},{12,4},{14,6},{1,9},{3,11}... | collective-permute-start | bytes 393224 | tf_op jit(solution)/shard_map/ppermute | solution.py:19
  17.1 4.4 %collective-permute-start.6 = (bf16[128,512]{1,0:T(8,128)(2,1)}, bf16[128,512]{1,0:T(8,128)(2,1)S(1)}, u32[]{:S(2)}, u32[]{:S(2)}) collective-permute-start(bf16[128,512]{1,0:T(8,128)(2,1)} %bitcast.54), channel_id=1, source_target_pairs={{0,10},{2,12},{4,14},{6,0},{8,2},{10,4},{12,6},{14,8},{1,11},{3,13... | collective-permute-start | bytes 393224 | tf_op jit(solution)/shard_map/ppermute | solution.py:19
  21.5 0.9 convert_reduce_fusion.1
  22.4 0.7 fusion.22
  23.1 0.0 copy-done
  23.1 1.0 convolution_convert_fusion
  24.1 0.6 reshape.61
  24.7 1.0 copy.11
  25.7 0.0 copy-start.1
  25.7 26.3 %all-to-all-start = ((bf16[128,24,128]{2,1,0:T(8,128)(2,1)}), bf16[128,24,128]{2,1,0:T(8,128)(2,1)S(1)}, u32[]{:S(2)}, u32[]{:S(2)}) async-start(bf16[128,24,128]{2,1,0:T(8,128)(2,1)} %bitcast.5), calls=%async_computation | async-start | bytes 1572864 | tf_op jit(solution)/shard_map/all_to_all | solution.py:23
  51.9 0.0 copy-start.2
  51.9 0.0 copy-done.1
  52.0 0.8 fusion.15
  52.8 0.1 broadcast_in_dim.67
  52.9 0.0 copy-done.2
  52.9 0.0 collective-permute-done.2
  52.9 5.1 %collective-permute-start.7 = (bf16[128,512]{1,0:T(8,128)(2,1)S(1)}, bf16[128,512]{1,0:T(8,128)(2,1)S(1)}, u32[]{:S(2)}, u32[]{:S(2)}) collective-permute-start(bf16[128,512]{1,0:T(8,128)(2,1)S(1)} %bitcast.55), channel_id=1, source_target_pairs={{0,12},{2,14},{4,0},{6,2},{8,4},{10,6},{12,8},{14,10},{1,13},{3,15... | collective-permute-start | bytes 393224 | tf_op jit(solution)/shard_map/ppermute | solution.py:19
  58.1 0.0 collective-permute-done.3
  58.1 3.1 %collective-permute-start.8 = (bf16[128,512]{1,0:T(8,128)(2,1)S(1)}, bf16[128,512]{1,0:T(8,128)(2,1)S(1)}, u32[]{:S(2)}, u32[]{:S(2)}) collective-permute-start(bf16[128,512]{1,0:T(8,128)(2,1)S(1)} %bitcast.56), channel_id=1, source_target_pairs={{0,14},{2,0},{4,2},{6,4},{8,6},{10,8},{12,10},{14,12},{1,15},{3,1}... | collective-permute-start | bytes 393224 | tf_op jit(solution)/shard_map/ppermute | solution.py:19
  61.2 0.0 collective-permute-done.4
  61.2 3.0 %collective-permute-start = (bf16[192,512]{1,0:T(8,128)(2,1)}, bf16[192,512]{1,0:T(8,128)(2,1)}, u32[]{:S(2)}, u32[]{:S(2)}) collective-permute-start(bf16[192,512]{1,0:T(8,128)(2,1)} %fusion.15), channel_id=1, source_target_pairs={{0,1},{1,0},{2,3},{3,2},{4,5},{5,4},{6,7},{7,6},{8,9},{9,8},{10,11... | collective-permute-start | bytes 589832 | tf_op jit(solution)/shard_map/ppermute | solution.py:14
  64.3 0.0 collective-permute-done.5
  64.3 0.0 collective-permute-done.6
  64.3 0.0 collective-permute-done.7
  64.4 1.7 %collective-permute-done.8 = bf16[128,512]{1,0:T(8,128)(2,1)S(1)} collective-permute-done((bf16[128,512]{1,0:T(8,128)(2,1)S(1)}, bf16[128,512]{1,0:T(8,128)(2,1)S(1)}, u32[]{:S(2)}, u32[]{:S(2)}) %collective-permute-start.8) | collective-permute-done | bytes 131104 | tf_op jit(solution)/shard_map/ppermute | solution.py:19
  66.1 11.6 %all-to-all-done = bf16[128,24,128]{2,1,0:T(8,128)(2,1)S(1)} async-done(((bf16[128,24,128]{2,1,0:T(8,128)(2,1)}), bf16[128,24,128]{2,1,0:T(8,128)(2,1)S(1)}, u32[]{:S(2)}, u32[]{:S(2)}) %all-to-all-start) | async-done | bytes 786464 | tf_op jit(solution)/shard_map/all_to_all | solution.py:23
  77.7 0.3 reshape.63
  78.0 0.6 fusion.25
  78.6 0.1 slice_select_fusion
  78.7 3.0 %collective-permute-start.9 = (f32[192,512]{1,0:T(8,128)S(1)}, f32[192,512]{1,0:T(8,128)S(1)}, u32[]{:S(2)}, u32[]{:S(2)}) collective-permute-start(f32[192,512]{1,0:T(8,128)S(1)} %slice_select_fusion), channel_id=1, source_target_pairs={{0,1},{1,0},{2,3},{3,2},{4,5},{5,4},{6,7},{7,6},{8,9},{9,8},{10,11... | collective-permute-start | bytes 1179656 | tf_op jit(solution)/shard_map/ppermute | solution.py:14
  81.7 0.0 collective-permute-done
  81.7 1.1 broadcast_select_fusion.1
  82.8 0.2 collective-permute-done.9
  83.0 0.2 multiply_reduce_fusion
  83.2 0.8 all_to_all.14
  84.0 4.6 %all-to-all-start.2 = ((f32[64,1,3]{2,1,0:T(1,128)}), f32[64,1,3]{2,1,0:T(1,128)S(1)}, u32[]{:S(2)}, u32[]{:S(2)}) async-start(f32[64,1,3]{2,1,0:T(1,128)} %bitcast.20), calls=%async_computation.2 | async-start | bytes 65536 | tf_op jit(solution)/shard_map/all_to_all | solution.py:23
  88.6 1.7 %convolution_convert_fusion.1 = bf16[1024,512]{1,0:T(8,128)(2,1)} fusion(bf16[384,1024]{1,0:T(8,128)(2,1)S(1)} %reshape.63, bf16[192,512]{1,0:T(8,128)(2,1)S(1)} %get-tuple-element.12, bf16[192,512]{1,0:T(8,128)(2,1)S(1)} %get-tuple-element.11), kind=kOutput, calls=%fused_computation.2 | convolution fusion | flops 403963904 | bytes 2228224 | tf_op jit(solution)/shard_map/dot_general | solution.py:84
  90.3 9.1 %all-to-all-done.2 = f32[64,1,3]{2,1,0:T(1,128)S(1)} async-done(((f32[64,1,3]{2,1,0:T(1,128)}), f32[64,1,3]{2,1,0:T(1,128)S(1)}, u32[]{:S(2)}, u32[]{:S(2)}) %all-to-all-start.2) | async-done | bytes 800 | tf_op jit(solution)/shard_map/all_to_all | solution.py:23
  99.4 5.4 %all-to-all-start.1 = ((bf16[8,128,512]{2,1,0:T(8,128)(2,1)}), bf16[8,128,512]{2,1,0:T(8,128)(2,1)S(1)}, u32[]{:S(2)}, u32[]{:S(2)}) async-start(bf16[8,128,512]{2,1,0:T(8,128)(2,1)} %bitcast.49), calls=%async_computation.1 | async-start | bytes 2097152 | tf_op jit(solution)/shard_map/all_to_all | solution.py:23
  104.8 0.2 fusion.17
  105.0 0.8 pad_maximum_fusion
  105.8 0.0 copy-start.3
  105.8 0.5 broadcast.17
  106.3 0.7 reduce.3
  107.0 0.1 broadcast_in_dim.75
  107.2 0.1 select_reduce_fusion
  107.3 26.7 %all-to-all-done.1 = bf16[8,128,512]{2,1,0:T(8,128)(2,1)S(1)} async-done(((bf16[8,128,512]{2,1,0:T(8,128)(2,1)}), bf16[8,128,512]{2,1,0:T(8,128)(2,1)S(1)}, u32[]{:S(2)}, u32[]{:S(2)}) %all-to-all-start.1) | async-done | bytes 1048608 | tf_op jit(solution)/shard_map/all_to_all | solution.py:23
  134.0 0.1 convert_reduce_fusion
  134.1 2.4 %collective-permute-start.1 = (bf16[128,512]{1,0:T(8,128)(2,1)S(1)}, bf16[128,512]{1,0:T(8,128)(2,1)S(1)}, u32[]{:S(2)}, u32[]{:S(2)}) collective-permute-start(bf16[128,512]{1,0:T(8,128)(2,1)S(1)} %convert_element_type.62), channel_id=1, source_target_pairs={{0,512},{16,528},{32,544},{48,560},{64,576},{80,592},{96,608},{112... | collective-permute-start | bytes 393224 | tf_op jit(solution)/shard_map/ppermute | solution.py:14
  136.6 0.0 copy-done.3
  136.6 0.5 bitcast_divide_fusion
  137.1 8.1 %collective-permute-done.1 = bf16[128,512]{1,0:T(8,128)(2,1)S(1)} collective-permute-done((bf16[128,512]{1,0:T(8,128)(2,1)S(1)}, bf16[128,512]{1,0:T(8,128)(2,1)S(1)}, u32[]{:S(2)}, u32[]{:S(2)}) %collective-permute-start.1) | collective-permute-done | bytes 131104 | tf_op jit(solution)/shard_map/ppermute | solution.py:14
  145.2 0.7 add_bitcast_fusion
  (9 shorter events, 0.1 us)
Async XLA Ops:
  0.6 22.5 %copy-start = (bf16[128,2048]{1,0:T(8,128)(2,1)S(1)}, bf16[128,2048]{1,0:T(8,128)(2,1)}, u32[]{:S(2)}) copy-start(bf16[128,2048]{1,0:T(8,128)(2,1)} %param.5) | copy-start | bytes 1572868
  0.6 52.2 %collective-permute-start.2 = (bf16[128,512]{1,0:T(8,128)(2,1)}, bf16[128,512]{1,0:T(8,128)(2,1)S(1)}, u32[]{:S(2)}, u32[]{:S(2)}) collective-permute-start(bf16[128,512]{1,0:T(8,128)(2,1)} %bitcast.50), channel_id=1, source_target_pairs={{0,2},{2,4},{4,6},{6,8},{8,10},{10,12},{12,14},{14,0},{1,3},{3,5},... | collective-permute-start | bytes 393224 | tf_op jit(solution)/shard_map/ppermute | solution.py:19
  4.7 53.4 %collective-permute-start.3 = (bf16[128,512]{1,0:T(8,128)(2,1)}, bf16[128,512]{1,0:T(8,128)(2,1)S(1)}, u32[]{:S(2)}, u32[]{:S(2)}) collective-permute-start(bf16[128,512]{1,0:T(8,128)(2,1)} %bitcast.51), channel_id=1, source_target_pairs={{0,4},{2,6},{4,8},{6,10},{8,12},{10,14},{12,0},{14,2},{1,5},{3,7},... | collective-permute-start | bytes 393224 | tf_op jit(solution)/shard_map/ppermute | solution.py:19
  8.8 52.4 %collective-permute-start.4 = (bf16[128,512]{1,0:T(8,128)(2,1)}, bf16[128,512]{1,0:T(8,128)(2,1)S(1)}, u32[]{:S(2)}, u32[]{:S(2)}) collective-permute-start(bf16[128,512]{1,0:T(8,128)(2,1)} %bitcast.52), channel_id=1, source_target_pairs={{0,6},{2,8},{4,10},{6,12},{8,14},{10,0},{12,2},{14,4},{1,7},{3,9},... | collective-permute-start | bytes 393224 | tf_op jit(solution)/shard_map/ppermute | solution.py:19
  13.2 51.1 %collective-permute-start.5 = (bf16[128,512]{1,0:T(8,128)(2,1)}, bf16[128,512]{1,0:T(8,128)(2,1)S(1)}, u32[]{:S(2)}, u32[]{:S(2)}) collective-permute-start(bf16[128,512]{1,0:T(8,128)(2,1)} %bitcast.53), channel_id=1, source_target_pairs={{0,8},{2,10},{4,12},{6,14},{8,0},{10,2},{12,4},{14,6},{1,9},{3,11}... | collective-permute-start | bytes 393224 | tf_op jit(solution)/shard_map/ppermute | solution.py:19
  17.1 47.2 %collective-permute-start.6 = (bf16[128,512]{1,0:T(8,128)(2,1)}, bf16[128,512]{1,0:T(8,128)(2,1)S(1)}, u32[]{:S(2)}, u32[]{:S(2)}) collective-permute-start(bf16[128,512]{1,0:T(8,128)(2,1)} %bitcast.54), channel_id=1, source_target_pairs={{0,10},{2,12},{4,14},{6,0},{8,2},{10,4},{12,6},{14,8},{1,11},{3,13... | collective-permute-start | bytes 393224 | tf_op jit(solution)/shard_map/ppermute | solution.py:19
  25.7 26.3 %copy-start.1 = (bf16[1,192,1024]{2,1,0:T(8,128)(2,1)S(1)}, bf16[1,192,1024]{2,1,0:T(8,128)(2,1)}, u32[]{:S(2)}) copy-start(bf16[1,192,1024]{2,1,0:T(8,128)(2,1)} %param.8) | copy-start | bytes 1179652
  25.7 52.0 %all-to-all-start = ((bf16[128,24,128]{2,1,0:T(8,128)(2,1)}), bf16[128,24,128]{2,1,0:T(8,128)(2,1)S(1)}, u32[]{:S(2)}, u32[]{:S(2)}) async-start(bf16[128,24,128]{2,1,0:T(8,128)(2,1)} %bitcast.5), calls=%async_computation | async-start | bytes 1572864 | tf_op jit(solution)/shard_map/all_to_all | solution.py:23
  51.9 0.9 copy-start.2
  52.9 11.4 %collective-permute-start.7 = (bf16[128,512]{1,0:T(8,128)(2,1)S(1)}, bf16[128,512]{1,0:T(8,128)(2,1)S(1)}, u32[]{:S(2)}, u32[]{:S(2)}) collective-permute-start(bf16[128,512]{1,0:T(8,128)(2,1)S(1)} %bitcast.55), channel_id=1, source_target_pairs={{0,12},{2,14},{4,0},{6,2},{8,4},{10,6},{12,8},{14,10},{1,13},{3,15... | collective-permute-start | bytes 393224 | tf_op jit(solution)/shard_map/ppermute | solution.py:19
  58.1 8.0 %collective-permute-start.8 = (bf16[128,512]{1,0:T(8,128)(2,1)S(1)}, bf16[128,512]{1,0:T(8,128)(2,1)S(1)}, u32[]{:S(2)}, u32[]{:S(2)}) collective-permute-start(bf16[128,512]{1,0:T(8,128)(2,1)S(1)} %bitcast.56), channel_id=1, source_target_pairs={{0,14},{2,0},{4,2},{6,4},{8,6},{10,8},{12,10},{14,12},{1,15},{3,1}... | collective-permute-start | bytes 393224 | tf_op jit(solution)/shard_map/ppermute | solution.py:19
  61.2 20.5 %collective-permute-start = (bf16[192,512]{1,0:T(8,128)(2,1)}, bf16[192,512]{1,0:T(8,128)(2,1)}, u32[]{:S(2)}, u32[]{:S(2)}) collective-permute-start(bf16[192,512]{1,0:T(8,128)(2,1)} %fusion.15), channel_id=1, source_target_pairs={{0,1},{1,0},{2,3},{3,2},{4,5},{5,4},{6,7},{7,6},{8,9},{9,8},{10,11... | collective-permute-start | bytes 589832 | tf_op jit(solution)/shard_map/ppermute | solution.py:14
  78.7 4.3 %collective-permute-start.9 = (f32[192,512]{1,0:T(8,128)S(1)}, f32[192,512]{1,0:T(8,128)S(1)}, u32[]{:S(2)}, u32[]{:S(2)}) collective-permute-start(f32[192,512]{1,0:T(8,128)S(1)} %slice_select_fusion), channel_id=1, source_target_pairs={{0,1},{1,0},{2,3},{3,2},{4,5},{5,4},{6,7},{7,6},{8,9},{9,8},{10,11... | collective-permute-start | bytes 1179656 | tf_op jit(solution)/shard_map/ppermute | solution.py:14
  84.0 15.4 %all-to-all-start.2 = ((f32[64,1,3]{2,1,0:T(1,128)}), f32[64,1,3]{2,1,0:T(1,128)S(1)}, u32[]{:S(2)}, u32[]{:S(2)}) async-start(f32[64,1,3]{2,1,0:T(1,128)} %bitcast.20), calls=%async_computation.2 | async-start | bytes 65536 | tf_op jit(solution)/shard_map/all_to_all | solution.py:23
  99.4 34.6 %all-to-all-start.1 = ((bf16[8,128,512]{2,1,0:T(8,128)(2,1)}), bf16[8,128,512]{2,1,0:T(8,128)(2,1)S(1)}, u32[]{:S(2)}, u32[]{:S(2)}) async-start(bf16[8,128,512]{2,1,0:T(8,128)(2,1)} %bitcast.49), calls=%async_computation.1 | async-start | bytes 2097152 | tf_op jit(solution)/shard_map/all_to_all | solution.py:23
  105.8 30.8 %copy-start.3 = (bf16[128,1]{0,1:T(2,128)(2,1)S(1)}, bf16[128,1]{0,1:T(2,128)(2,1)}, u32[]{:S(2)}) copy-start(bf16[128,1]{0,1:T(2,128)(2,1)} %param.6) | copy-start | bytes 772
  134.1 11.0 %collective-permute-start.1 = (bf16[128,512]{1,0:T(8,128)(2,1)S(1)}, bf16[128,512]{1,0:T(8,128)(2,1)S(1)}, u32[]{:S(2)}, u32[]{:S(2)}) collective-permute-start(bf16[128,512]{1,0:T(8,128)(2,1)S(1)} %convert_element_type.62), channel_id=1, source_target_pairs={{0,512},{16,528},{32,544},{48,560},{64,576},{80,592},{96,608},{112... | collective-permute-start | bytes 393224 | tf_op jit(solution)/shard_map/ppermute | solution.py:14

commit v2 on v1

--- a/solution.py
+++ b/solution.py
@@ -14,9 +14,14 @@
     return lax.ppermute(block, axis, [(k, k ^ bit) for k in range(count)])
 
 
-def shift(block, axis, step):
-    count = lax.axis_size(axis)
-    return lax.ppermute(block, axis, [(k, (k + step) % count) for k in range(count)])
+def fan(block, step):
+    chips = lax.axis_size("x")
+    route = [
+        (chip * 2 + core, (chip + step - 2 * step * core) % chips * 2 + core)
+        for chip in range(chips)
+        for core in range(2)
+    ]
+    return lax.ppermute(block, ("x", "core"), route)
 
 
 def exchange(blocks, axis):
@@ -62,12 +67,24 @@
     scaled = got.reshape(2 * rows, chips * lanes)
 
     chip = lax.axis_index("x")
+    ahead = jnp.where(first, -1, 1)
+    mate = swap(down_weight[0], "core", 1)
+    pair = jnp.concatenate([down_weight, mate[None]], axis=0)
+    pieces = {0: down_weight[0]}
+    relayed = []
+    for step in range(1, chips // 2):
+        got_pair = fan(pair, step)
+        pieces[step] = got_pair[0]
+        relayed.append(got_pair[1])
+    far = fan(down_weight[0], chips // 2)
+    pieces[chips // 2] = far
+    relayed = swap(jnp.stack(relayed), "core", 1)
+    for step in range(1, chips // 2):
+        pieces[-step] = relayed[step - 1]
     weight = jnp.zeros((chips,) + down_weight.shape[1:], BF)
-    weight = lax.dynamic_update_index_in_dim(weight, down_weight[0], chip, 0)
-    for step in range(1, chips):
-        block = shift(down_weight[0], "x", step)
+    for step, piece in pieces.items():
         weight = lax.dynamic_update_index_in_dim(
-            weight, block, jnp.bitwise_and(chip - step, chips - 1), 0
+            weight, piece, jnp.bitwise_and(chip + ahead * step, chips - 1), 0
         )
     weight = weight.reshape(chips * lanes, ff)
 

time: 147 us -> 150 us (1.020)
  starting transfers between devices: 73.8 us -> 81 us
  waiting for transfers between devices: 57.4 us -> 51.2 us
  local copies, waits for them, and re-layouts: 3.52 us -> 5.05 us
    ppermute x3 -> x5, starting transfers between devices: 8.47 us -> 32.4 us  [swap(): return lax.ppermute(block, axis, [(k, k ^ bit) for k in range(count)])]
    ppermute x7 -> x4, starting transfers between devices: 29 us -> 10.8 us  [fan(): return lax.ppermute(block, ('x', 'core'), route)]
    all_to_all x3, waiting for transfers between devices: 47.3 us -> 36 us  [exchange(): return lax.all_to_all(blocks, axis, split_axis=0, concat_axis=0, tiled=True)]
    ppermute x7 -> x4, waiting for transfers between devices: 1.75 us -> 6.98 us  [fan(): return lax.ppermute(block, ('x', 'core'), route)]
    all_to_all x3, starting transfers between devices: 36.2 us -> 37.8 us  [exchange(): return lax.all_to_all(blocks, axis, split_axis=0, concat_axis=0, tiled=True)]
    ppermute x3 -> x5, waiting for transfers between devices: 8.27 us -> 8.28 us  [swap(): return lax.ppermute(block, axis, [(k, k ^ bit) for k in range(count)])]
  transfers between devices with their start and end apart: 13 -> 12, of which waited for: 6 -> 7; matrix products, arithmetic and copies ran while one was open for 8% -> 9% of each run, Pallas kernels for 0% -> 0%
where the time goes in v2:
time: 150 us
  starting transfers between devices  81 us (54%)
  waiting for transfers between devices  51.2 us (34%)
  other arithmetic  8.03 us (5%)
  local copies, waits for them, and re-layouts  5.05 us (3%)
  matrix products  3.31 us (2%)
    all_to_all x3, starting transfers between devices, exchange(): return lax.all_to_all(blocks, axis, split_axis=0, concat_axis=0, tiled=True)  37.8 us
    all_to_all x3, waiting for transfers between devices, exchange(): return lax.all_to_all(blocks, axis, split_axis=0, concat_axis=0, tiled=True)  36 us
    ppermute x5, starting transfers between devices, swap(): return lax.ppermute(block, axis, [(k, k ^ bit) for k in range(count)])  32.4 us
    ppermute x4, starting transfers between devices, fan(): return lax.ppermute(block, ('x', 'core'), route)  10.8 us
    ppermute x5, waiting for transfers between devices, swap(): return lax.ppermute(block, axis, [(k, k ^ bit) for k in range(count)])  8.28 us
    ppermute x4, waiting for transfers between devices, fan(): return lax.ppermute(block, ('x', 'core'), route)  6.98 us
  transfers between devices with their start and end apart: 12, of which 7 were waited for; matrix products, arithmetic and copies ran while one was open for 9% of the time, Pallas kernels for 0%

profile of v2, /device:TPU:1, one launch (start us, length us, event | category | flops | bytes accessed | tf_op | source)
XLA Modules:
  0.0 149.6 jit_solution(11993982455064846073)
XLA Ops:
  0.6 0.0 copy-start
  0.6 17.6 %collective-permute-start.2 = (bf16[128,512]{1,0:T(8,128)(2,1)}, bf16[128,512]{1,0:T(8,128)(2,1)S(1)}, u32[]{:S(2)}, u32[]{:S(2)}) collective-permute-start(bf16[128,512]{1,0:T(8,128)(2,1)} %bitcast.39), channel_id=1, source_target_pairs={{0,1},{1,0},{2,3},{3,2},{4,5},{5,4},{6,7},{7,6},{8,9},{9,8},{10,11... | collective-permute-start | bytes 393224 | tf_op jit(solution)/shard_map/ppermute | solution.py:14
  18.2 1.9 %collective-permute-start.6 = (bf16[128,512]{1,0:T(8,128)(2,1)}, bf16[128,512]{1,0:T(8,128)(2,1)}, u32[]{:S(2)}, u32[]{:S(2)}) collective-permute-start(bf16[128,512]{1,0:T(8,128)(2,1)} %bitcast.40), channel_id=1, source_target_pairs={{0,8},{1,9},{2,10},{3,11},{4,12},{5,13},{6,14},{7,15},{8,0},{9,1},... | collective-permute-start | bytes 393224 | tf_op jit(solution)/shard_map/ppermute | solution.py:24
  20.1 0.9 convert_reduce_fusion.1
  21.0 0.7 fusion.22
  21.7 0.0 collective-permute-done.2
  21.7 0.9 pad_maximum_fusion.2
  22.6 1.9 %collective-permute-start.3 = (bf16[2,128,512]{2,1,0:T(8,128)(2,1)S(1)}, bf16[2,128,512]{2,1,0:T(8,128)(2,1)S(1)}, u32[]{:S(2)}, u32[]{:S(2)}) collective-permute-start(bf16[2,128,512]{2,1,0:T(8,128)(2,1)S(1)} %pad_maximum_fusion.2), channel_id=1, source_target_pairs={{0,2},{1,15},{2,4},{3,1},{4,6},{5,3},{6,8},{7,5},{8,10},{9,7},{10,... | collective-permute-start | bytes 786440 | tf_op jit(solution)/shard_map/ppermute | solution.py:24
  24.6 0.0 copy-done
  24.6 1.0 convolution_convert_fusion
  25.6 0.6 reshape.61
  26.2 1.0 copy.11
  27.2 0.0 copy-start.2
  27.2 21.3 %all-to-all-start = ((bf16[128,24,128]{2,1,0:T(8,128)(2,1)}), bf16[128,24,128]{2,1,0:T(8,128)(2,1)S(1)}, u32[]{:S(2)}, u32[]{:S(2)}) async-start(bf16[128,24,128]{2,1,0:T(8,128)(2,1)} %bitcast.5), calls=%async_computation | async-start | bytes 1572864 | tf_op jit(solution)/shard_map/all_to_all | solution.py:28
  48.4 1.9 %collective-permute-start.4 = (bf16[2,128,512]{2,1,0:T(8,128)(2,1)S(1)}, bf16[2,128,512]{2,1,0:T(8,128)(2,1)S(1)}, u32[]{:S(2)}, u32[]{:S(2)}) collective-permute-start(bf16[2,128,512]{2,1,0:T(8,128)(2,1)S(1)} %pad_maximum_fusion.2), channel_id=1, source_target_pairs={{0,4},{1,13},{2,6},{3,15},{4,8},{5,1},{6,10},{7,3},{8,12},{9,5},{1... | collective-permute-start | bytes 786440 | tf_op jit(solution)/shard_map/ppermute | solution.py:24
  50.4 0.1 broadcast_in_dim.58
  50.5 0.0 copy-done.2
  50.5 5.0 %collective-permute-start.5 = (bf16[2,128,512]{2,1,0:T(8,128)(2,1)S(1)}, bf16[2,128,512]{2,1,0:T(8,128)(2,1)S(1)}, u32[]{:S(2)}, u32[]{:S(2)}) collective-permute-start(bf16[2,128,512]{2,1,0:T(8,128)(2,1)S(1)} %pad_maximum_fusion.2), channel_id=1, source_target_pairs={{0,6},{1,11},{2,8},{3,13},{4,10},{5,15},{6,12},{7,1},{8,14},{9,3},... | collective-permute-start | bytes 786440 | tf_op jit(solution)/shard_map/ppermute | solution.py:24
  55.5 0.0 collective-permute-done.3
  55.6 0.0 copy-start.1
  55.6 3.9 %collective-permute-done.4 = bf16[2,128,512]{2,1,0:T(8,128)(2,1)S(1)} collective-permute-done((bf16[2,128,512]{2,1,0:T(8,128)(2,1)S(1)}, bf16[2,128,512]{2,1,0:T(8,128)(2,1)S(1)}, u32[]{:S(2)}, u32[]{:S(2)}) %collective-permute-start.4) | collective-permute-done | bytes 262176 | tf_op jit(solution)/shard_map/ppermute | solution.py:24
  59.5 3.0 %collective-permute-done.5 = bf16[2,128,512]{2,1,0:T(8,128)(2,1)S(1)} collective-permute-done((bf16[2,128,512]{2,1,0:T(8,128)(2,1)S(1)}, bf16[2,128,512]{2,1,0:T(8,128)(2,1)S(1)}, u32[]{:S(2)}, u32[]{:S(2)}) %collective-permute-start.5) | collective-permute-done | bytes 262176 | tf_op jit(solution)/shard_map/ppermute | solution.py:24
  62.7 7.5 %collective-permute-start.7 = (bf16[3,128,512]{2,1,0:T(8,128)(2,1)S(1)}, bf16[3,128,512]{2,1,0:T(8,128)(2,1)S(1)}, u32[]{:S(2)}, u32[]{:S(2)}) collective-permute-start(bf16[3,128,512]{2,1,0:T(8,128)(2,1)S(1)} %pad_maximum_fusion), channel_id=1, source_target_pairs={{0,1},{1,0},{2,3},{3,2},{4,5},{5,4},{6,7},{7,6},{8,9},{9,8},{10,11... | collective-permute-start | bytes 1179656 | tf_op jit(solution)/shard_map/ppermute | solution.py:14
  70.2 0.0 copy-done.1
  70.2 0.8 fusion.15
  71.0 1.9 %collective-permute-start = (bf16[192,512]{1,0:T(8,128)(2,1)}, bf16[192,512]{1,0:T(8,128)(2,1)}, u32[]{:S(2)}, u32[]{:S(2)}) collective-permute-start(bf16[192,512]{1,0:T(8,128)(2,1)} %fusion.15), channel_id=1, source_target_pairs={{0,1},{1,0},{2,3},{3,2},{4,5},{5,4},{6,7},{7,6},{8,9},{9,8},{10,11... | collective-permute-start | bytes 589832 | tf_op jit(solution)/shard_map/ppermute | solution.py:14
  72.9 0.0 collective-permute-done.6
  72.9 0.9 bitcast_dynamic-update-slice_fusion
  73.9 0.0 collective-permute-done.7
  73.9 0.2 all-to-all-done
  74.2 0.3 reshape.63
  74.5 0.6 fusion.28
  75.1 0.1 slice_select_fusion
  75.1 3.0 %collective-permute-start.8 = (f32[192,512]{1,0:T(8,128)S(1)}, f32[192,512]{1,0:T(8,128)S(1)}, u32[]{:S(2)}, u32[]{:S(2)}) collective-permute-start(f32[192,512]{1,0:T(8,128)S(1)} %slice_select_fusion), channel_id=1, source_target_pairs={{0,1},{1,0},{2,3},{3,2},{4,5},{5,4},{6,7},{7,6},{8,9},{9,8},{10,11... | collective-permute-start | bytes 1179656 | tf_op jit(solution)/shard_map/ppermute | solution.py:14
  78.2 0.0 collective-permute-done
  78.2 1.1 broadcast_select_fusion.1
  79.3 0.2 collective-permute-done.8
  79.5 0.2 multiply_reduce_fusion
  79.7 0.8 all_to_all.14
  80.5 11.2 %all-to-all-start.2 = ((f32[64,1,3]{2,1,0:T(1,128)}), f32[64,1,3]{2,1,0:T(1,128)S(1)}, u32[]{:S(2)}, u32[]{:S(2)}) async-start(f32[64,1,3]{2,1,0:T(1,128)} %bitcast.15), calls=%async_computation.2 | async-start | bytes 65536 | tf_op jit(solution)/shard_map/all_to_all | solution.py:28
  91.7 1.7 %convolution_convert_fusion.1 = bf16[1024,512]{1,0:T(8,128)(2,1)} fusion(bf16[384,1024]{1,0:T(8,128)(2,1)S(1)} %reshape.63, bf16[192,512]{1,0:T(8,128)(2,1)S(1)} %get-tuple-element.12, bf16[192,512]{1,0:T(8,128)(2,1)S(1)} %get-tuple-element.11), kind=kOutput, calls=%fused_computation.2 | convolution fusion | flops 403963904 | bytes 2228224 | tf_op jit(solution)/shard_map/dot_general | solution.py:101
  93.4 9.1 %all-to-all-done.2 = f32[64,1,3]{2,1,0:T(1,128)S(1)} async-done(((f32[64,1,3]{2,1,0:T(1,128)}), f32[64,1,3]{2,1,0:T(1,128)S(1)}, u32[]{:S(2)}, u32[]{:S(2)}) %all-to-all-start.2) | async-done | bytes 800 | tf_op jit(solution)/shard_map/all_to_all | solution.py:28
  102.5 0.0 copy-start.3
  102.5 0.6 copy-done.3
  103.1 5.4 %all-to-all-start.1 = ((bf16[8,128,512]{2,1,0:T(8,128)(2,1)}), bf16[8,128,512]{2,1,0:T(8,128)(2,1)S(1)}, u32[]{:S(2)}, u32[]{:S(2)}) async-start(bf16[8,128,512]{2,1,0:T(8,128)(2,1)} %bitcast.38), calls=%async_computation.1 | async-start | bytes 2097152 | tf_op jit(solution)/shard_map/all_to_all | solution.py:28
  108.5 0.0 copy-start.4
  108.5 0.2 fusion.17
  108.7 0.8 pad_maximum_fusion.1
  109.5 0.0 copy-start.5
  109.5 0.5 broadcast.17
  110.0 0.0 copy-done.4
  110.0 0.7 reduce.3
  110.7 0.1 broadcast_in_dim.61
  110.9 0.1 select_reduce_fusion
  111.0 26.7 %all-to-all-done.1 = bf16[8,128,512]{2,1,0:T(8,128)(2,1)S(1)} async-done(((bf16[8,128,512]{2,1,0:T(8,128)(2,1)}), bf16[8,128,512]{2,1,0:T(8,128)(2,1)S(1)}, u32[]{:S(2)}, u32[]{:S(2)}) %all-to-all-start.1) | async-done | bytes 1048608 | tf_op jit(solution)/shard_map/all_to_all | solution.py:28
  137.7 0.1 convert_reduce_fusion
  137.8 2.4 %collective-permute-start.1 = (bf16[128,512]{1,0:T(8,128)(2,1)S(1)}, bf16[128,512]{1,0:T(8,128)(2,1)S(1)}, u32[]{:S(2)}, u32[]{:S(2)}) collective-permute-start(bf16[128,512]{1,0:T(8,128)(2,1)S(1)} %convert_element_type.62), channel_id=1, source_target_pairs={{0,512},{16,528},{32,544},{48,560},{64,576},{80,592},{96,608},{112... | collective-permute-start | bytes 393224 | tf_op jit(solution)/shard_map/ppermute | solution.py:14
  140.3 0.0 copy-done.5
  140.3 0.5 bitcast_divide_fusion
  140.8 8.1 %collective-permute-done.1 = bf16[128,512]{1,0:T(8,128)(2,1)S(1)} collective-permute-done((bf16[128,512]{1,0:T(8,128)(2,1)S(1)}, bf16[128,512]{1,0:T(8,128)(2,1)S(1)}, u32[]{:S(2)}, u32[]{:S(2)}) %collective-permute-start.1) | collective-permute-done | bytes 131104 | tf_op jit(solution)/shard_map/ppermute | solution.py:14
  148.9 0.7 add_bitcast_fusion
  (9 shorter events, 0.2 us)
Async XLA Ops:
  0.6 24.0 %copy-start = (bf16[128,2048]{1,0:T(8,128)(2,1)S(1)}, bf16[128,2048]{1,0:T(8,128)(2,1)}, u32[]{:S(2)}) copy-start(bf16[128,2048]{1,0:T(8,128)(2,1)} %param.5) | copy-start | bytes 1572868
  0.6 21.1 %collective-permute-start.2 = (bf16[128,512]{1,0:T(8,128)(2,1)}, bf16[128,512]{1,0:T(8,128)(2,1)S(1)}, u32[]{:S(2)}, u32[]{:S(2)}) collective-permute-start(bf16[128,512]{1,0:T(8,128)(2,1)} %bitcast.39), channel_id=1, source_target_pairs={{0,1},{1,0},{2,3},{3,2},{4,5},{5,4},{6,7},{7,6},{8,9},{9,8},{10,11... | collective-permute-start | bytes 393224 | tf_op jit(solution)/shard_map/ppermute | solution.py:14
  18.2 54.7 %collective-permute-start.6 = (bf16[128,512]{1,0:T(8,128)(2,1)}, bf16[128,512]{1,0:T(8,128)(2,1)}, u32[]{:S(2)}, u32[]{:S(2)}) collective-permute-start(bf16[128,512]{1,0:T(8,128)(2,1)} %bitcast.40), channel_id=1, source_target_pairs={{0,8},{1,9},{2,10},{3,11},{4,12},{5,13},{6,14},{7,15},{8,0},{9,1},... | collective-permute-start | bytes 393224 | tf_op jit(solution)/shard_map/ppermute | solution.py:24
  22.6 32.9 %collective-permute-start.3 = (bf16[2,128,512]{2,1,0:T(8,128)(2,1)S(1)}, bf16[2,128,512]{2,1,0:T(8,128)(2,1)S(1)}, u32[]{:S(2)}, u32[]{:S(2)}) collective-permute-start(bf16[2,128,512]{2,1,0:T(8,128)(2,1)S(1)} %pad_maximum_fusion.2), channel_id=1, source_target_pairs={{0,2},{1,15},{2,4},{3,1},{4,6},{5,3},{6,8},{7,5},{8,10},{9,7},{10,... | collective-permute-start | bytes 786440 | tf_op jit(solution)/shard_map/ppermute | solution.py:24
  27.2 23.3 %copy-start.2 = (bf16[1,128,512]{2,1,0:T(8,128)(2,1)S(1)}, bf16[1,128,512]{2,1,0:T(8,128)(2,1)}, u32[]{:S(2)}) copy-start(bf16[1,128,512]{2,1,0:T(8,128)(2,1)} %param.9) | copy-start | bytes 393220
  27.2 47.0 %all-to-all-start = ((bf16[128,24,128]{2,1,0:T(8,128)(2,1)}), bf16[128,24,128]{2,1,0:T(8,128)(2,1)S(1)}, u32[]{:S(2)}, u32[]{:S(2)}) async-start(bf16[128,24,128]{2,1,0:T(8,128)(2,1)} %bitcast.5), calls=%async_computation | async-start | bytes 1572864 | tf_op jit(solution)/shard_map/all_to_all | solution.py:28
  48.4 11.1 %collective-permute-start.4 = (bf16[2,128,512]{2,1,0:T(8,128)(2,1)S(1)}, bf16[2,128,512]{2,1,0:T(8,128)(2,1)S(1)}, u32[]{:S(2)}, u32[]{:S(2)}) collective-permute-start(bf16[2,128,512]{2,1,0:T(8,128)(2,1)S(1)} %pad_maximum_fusion.2), channel_id=1, source_target_pairs={{0,4},{1,13},{2,6},{3,15},{4,8},{5,1},{6,10},{7,3},{8,12},{9,5},{1... | collective-permute-start | bytes 786440 | tf_op jit(solution)/shard_map/ppermute | solution.py:24
  50.5 12.1 %collective-permute-start.5 = (bf16[2,128,512]{2,1,0:T(8,128)(2,1)S(1)}, bf16[2,128,512]{2,1,0:T(8,128)(2,1)S(1)}, u32[]{:S(2)}, u32[]{:S(2)}) collective-permute-start(bf16[2,128,512]{2,1,0:T(8,128)(2,1)S(1)} %pad_maximum_fusion.2), channel_id=1, source_target_pairs={{0,6},{1,11},{2,8},{3,13},{4,10},{5,15},{6,12},{7,1},{8,14},{9,3},... | collective-permute-start | bytes 786440 | tf_op jit(solution)/shard_map/ppermute | solution.py:24
  55.6 14.6 %copy-start.1 = (bf16[1,192,1024]{2,1,0:T(8,128)(2,1)S(1)}, bf16[1,192,1024]{2,1,0:T(8,128)(2,1)}, u32[]{:S(2)}) copy-start(bf16[1,192,1024]{2,1,0:T(8,128)(2,1)} %param.8) | copy-start | bytes 1179652
  62.7 11.2 %collective-permute-start.7 = (bf16[3,128,512]{2,1,0:T(8,128)(2,1)S(1)}, bf16[3,128,512]{2,1,0:T(8,128)(2,1)S(1)}, u32[]{:S(2)}, u32[]{:S(2)}) collective-permute-start(bf16[3,128,512]{2,1,0:T(8,128)(2,1)S(1)} %pad_maximum_fusion), channel_id=1, source_target_pairs={{0,1},{1,0},{2,3},{3,2},{4,5},{5,4},{6,7},{7,6},{8,9},{9,8},{10,11... | collective-permute-start | bytes 1179656 | tf_op jit(solution)/shard_map/ppermute | solution.py:14
  71.0 7.2 %collective-permute-start = (bf16[192,512]{1,0:T(8,128)(2,1)}, bf16[192,512]{1,0:T(8,128)(2,1)}, u32[]{:S(2)}, u32[]{:S(2)}) collective-permute-start(bf16[192,512]{1,0:T(8,128)(2,1)} %fusion.15), channel_id=1, source_target_pairs={{0,1},{1,0},{2,3},{3,2},{4,5},{5,4},{6,7},{7,6},{8,9},{9,8},{10,11... | collective-permute-start | bytes 589832 | tf_op jit(solution)/shard_map/ppermute | solution.py:14
  75.1 4.3 %collective-permute-start.8 = (f32[192,512]{1,0:T(8,128)S(1)}, f32[192,512]{1,0:T(8,128)S(1)}, u32[]{:S(2)}, u32[]{:S(2)}) collective-permute-start(f32[192,512]{1,0:T(8,128)S(1)} %slice_select_fusion), channel_id=1, source_target_pairs={{0,1},{1,0},{2,3},{3,2},{4,5},{5,4},{6,7},{7,6},{8,9},{9,8},{10,11... | collective-permute-start | bytes 1179656 | tf_op jit(solution)/shard_map/ppermute | solution.py:14
  80.5 22.0 %all-to-all-start.2 = ((f32[64,1,3]{2,1,0:T(1,128)}), f32[64,1,3]{2,1,0:T(1,128)S(1)}, u32[]{:S(2)}, u32[]{:S(2)}) async-start(f32[64,1,3]{2,1,0:T(1,128)} %bitcast.15), calls=%async_computation.2 | async-start | bytes 65536 | tf_op jit(solution)/shard_map/all_to_all | solution.py:28
  102.5 0.6 copy-start.3
  103.1 34.6 %all-to-all-start.1 = ((bf16[8,128,512]{2,1,0:T(8,128)(2,1)}), bf16[8,128,512]{2,1,0:T(8,128)(2,1)S(1)}, u32[]{:S(2)}, u32[]{:S(2)}) async-start(bf16[8,128,512]{2,1,0:T(8,128)(2,1)} %bitcast.38), calls=%async_computation.1 | async-start | bytes 2097152 | tf_op jit(solution)/shard_map/all_to_all | solution.py:28
  108.5 1.5 %copy-start.4 = (f32[64,1,3]{2,1,0:T(1,128)S(1)}, f32[64,1,3]{2,1,0:T(1,128)}, u32[]{:S(2)}) copy-start(f32[64,1,3]{2,1,0:T(1,128)} %copy-done.3) | copy-start | bytes 2308
  109.5 30.8 %copy-start.5 = (bf16[128,1]{0,1:T(2,128)(2,1)S(1)}, bf16[128,1]{0,1:T(2,128)(2,1)}, u32[]{:S(2)}) copy-start(bf16[128,1]{0,1:T(2,128)(2,1)} %param.6) | copy-start | bytes 772
  137.8 11.0 %collective-permute-start.1 = (bf16[128,512]{1,0:T(8,128)(2,1)S(1)}, bf16[128,512]{1,0:T(8,128)(2,1)S(1)}, u32[]{:S(2)}, u32[]{:S(2)}) collective-permute-start(bf16[128,512]{1,0:T(8,128)(2,1)S(1)} %convert_element_type.62), channel_id=1, source_target_pairs={{0,512},{16,528},{32,544},{48,560},{64,576},{80,592},{96,608},{112... | collective-permute-start | bytes 393224 | tf_op jit(solution)/shard_map/ppermute | solution.py:14

commit v3 on v2

--- a/solution.py
+++ b/solution.py
@@ -1,5 +1,6 @@
 import jax
 import jax.numpy as jnp
+import numpy as np
 from jax import lax
 from jax.sharding import Mesh, PartitionSpec as P
 
@@ -14,10 +15,10 @@
     return lax.ppermute(block, axis, [(k, k ^ bit) for k in range(count)])
 
 
-def fan(block, step):
+def fan(block):
     chips = lax.axis_size("x")
     route = [
-        (chip * 2 + core, (chip + step - 2 * step * core) % chips * 2 + core)
+        (chip * 2 + core, (chip + 1 - 2 * core) % chips * 2 + core)
         for chip in range(chips)
         for core in range(2)
     ]
@@ -54,8 +55,10 @@
         jnp.arange(tokens)[None, :] < jnp.arange(tokens)[:, None]
     )
     position = jnp.sum(same.astype(jnp.int32), axis=1)
-    target = ids * cap + position
-    place = target[:, None] == jnp.arange(rows, dtype=jnp.int32)[None, :]
+    row = np.arange(rows, dtype=np.int32)
+    place = (ids[:, None] == (row // cap)[None, :]) & (
+        position[:, None] == (row % cap)[None, :]
+    )
     probs = router_probs.astype(F32)
     spread = jnp.where(place, probs, 0.0).astype(BF)
     sent = lax.dot_general(
@@ -72,12 +75,13 @@
     pair = jnp.concatenate([down_weight, mate[None]], axis=0)
     pieces = {0: down_weight[0]}
     relayed = []
+    moving = pair
     for step in range(1, chips // 2):
-        got_pair = fan(pair, step)
-        pieces[step] = got_pair[0]
-        relayed.append(got_pair[1])
-    far = fan(down_weight[0], chips // 2)
-    pieces[chips // 2] = far
+        moving = fan(moving)
+        pieces[step] = moving[0]
+        relayed.append(moving[1])
+    far = fan(moving)
+    pieces[chips // 2] = far[0]
     relayed = swap(jnp.stack(relayed), "core", 1)
     for step in range(1, chips // 2):
         pieces[-step] = relayed[step - 1]

time: 150 us -> 144 us (0.960)
  starting transfers between devices: 81 us -> 65.6 us
  waiting for transfers between devices: 51.2 us -> 59.5 us
    all_to_all x3, starting transfers between devices: 37.8 us -> 26.6 us  [exchange(): return lax.all_to_all(blocks, axis, split_axis=0, concat_axis=0, tiled=True)]
    ppermute x5, starting transfers between devices: 32.4 us -> 25.9 us  [swap(): return lax.ppermute(block, axis, [(k, k ^ bit) for k in range(count)])]
    all_to_all x3, waiting for transfers between devices: 36 us -> 41.7 us  [exchange(): return lax.all_to_all(blocks, axis, split_axis=0, concat_axis=0, tiled=True)]
    ppermute x4, starting transfers between devices: 10.8 us -> 13.2 us  [fan(): return lax.ppermute(block, ('x', 'core'), route)]
  transfers between devices with their start and end apart: 12 -> 12, of which waited for: 7 -> 8; matrix products, arithmetic and copies ran while one was open for 9% -> 9% of each run, Pallas kernels for 0% -> 0%
where the time goes in v3:
time: 144 us; the launch traced here: 143 us
  starting transfers between devices  65.6 us (46%)
  waiting for transfers between devices  59.5 us (41%)
  other arithmetic  7.4 us (5%)
  local copies, waits for them, and re-layouts  6.08 us (4%)
  matrix products  3.43 us (2%)
    all_to_all x3, waiting for transfers between devices, exchange(): return lax.all_to_all(blocks, axis, split_axis=0, concat_axis=0, tiled=True)  41.7 us
    all_to_all x3, starting transfers between devices, exchange(): return lax.all_to_all(blocks, axis, split_axis=0, concat_axis=0, tiled=True)  26.6 us
    ppermute x5, starting transfers between devices, swap(): return lax.ppermute(block, axis, [(k, k ^ bit) for k in range(count)])  25.9 us
    ppermute x4, starting transfers between devices, fan(): return lax.ppermute(block, ('x', 'core'), route)  13.2 us
    ppermute x5, waiting for transfers between devices, swap(): return lax.ppermute(block, axis, [(k, k ^ bit) for k in range(count)])  9.45 us
    ppermute x4, waiting for transfers between devices, fan(): return lax.ppermute(block, ('x', 'core'), route)  8.35 us
  transfers between devices with their start and end apart: 12, of which 8 were waited for; matrix products, arithmetic and copies ran while one was open for 9% of the time, Pallas kernels for 0%

profile of v3, /device:TPU:1, one launch (start us, length us, event | category | flops | bytes accessed | tf_op | source)
XLA Modules:
  0.0 143.1 jit_solution(14565633373611842329)
XLA Ops:
  0.6 0.0 copy-start
  0.6 16.2 %collective-permute-start.2 = (bf16[128,512]{1,0:T(8,128)(2,1)}, bf16[128,512]{1,0:T(8,128)(2,1)S(1)}, u32[]{:S(2)}, u32[]{:S(2)}) collective-permute-start(bf16[128,512]{1,0:T(8,128)(2,1)} %bitcast.31), channel_id=1, source_target_pairs={{0,1},{1,0},{2,3},{3,2},{4,5},{5,4},{6,7},{7,6},{8,9},{9,8},{10,11... | collective-permute-start | bytes 393224 | tf_op jit(solution)/shard_map/ppermute | solution.py:15
  16.8 1.2 collective-permute-done.2
  18.0 0.9 pad_maximum_fusion.2
  18.9 1.9 %collective-permute-start.3 = (bf16[2,128,512]{2,1,0:T(8,128)(2,1)S(1)}, bf16[2,128,512]{2,1,0:T(8,128)(2,1)S(1)}, u32[]{:S(2)}, u32[]{:S(2)}) collective-permute-start(bf16[2,128,512]{2,1,0:T(8,128)(2,1)S(1)} %pad_maximum_fusion.2), channel_id=1, source_target_pairs={{0,2},{1,15},{2,4},{3,1},{4,6},{5,3},{6,8},{7,5},{8,10},{9,7},{10,... | collective-permute-start | bytes 786440 | tf_op jit(solution)/shard_map/ppermute | solution.py:25
  20.8 0.9 convert_reduce_fusion.1
  21.8 4.6 %collective-permute-done.3 = bf16[2,128,512]{2,1,0:T(8,128)(2,1)S(1)} collective-permute-done((bf16[2,128,512]{2,1,0:T(8,128)(2,1)S(1)}, bf16[2,128,512]{2,1,0:T(8,128)(2,1)S(1)}, u32[]{:S(2)}, u32[]{:S(2)}) %collective-permute-start.3) | collective-permute-done | bytes 262176 | tf_op jit(solution)/shard_map/ppermute | solution.py:25
  26.3 2.8 %collective-permute-start.4 = (bf16[2,128,512]{2,1,0:T(8,128)(2,1)S(1)}, bf16[2,128,512]{2,1,0:T(8,128)(2,1)S(1)}, u32[]{:S(2)}, u32[]{:S(2)}) collective-permute-start(bf16[2,128,512]{2,1,0:T(8,128)(2,1)S(1)} %collective-permute-done.3), channel_id=1, source_target_pairs={{0,2},{1,15},{2,4},{3,1},{4,6},{5,3},{6,8},{7,5},{8,10},{9,7},{10,... | collective-permute-start | bytes 786440 | tf_op jit(solution)/shard_map/ppermute | solution.py:25
  29.2 0.0 copy-done
  29.2 1.1 convolution_convert_fusion
  30.3 0.6 reshape.60
  30.9 1.0 copy.13
  31.9 14.3 %all-to-all-start = ((bf16[128,24,128]{2,1,0:T(8,128)(2,1)}), bf16[128,24,128]{2,1,0:T(8,128)(2,1)S(1)}, u32[]{:S(2)}, u32[]{:S(2)}) async-start(bf16[128,24,128]{2,1,0:T(8,128)(2,1)} %bitcast.3), calls=%async_computation | async-start | bytes 1572864 | tf_op jit(solution)/shard_map/all_to_all | solution.py:29
  46.2 0.1 broadcast_in_dim.55
  46.3 0.0 copy-done.2
  46.3 0.0 collective-permute-done.4
  46.3 3.7 %collective-permute-start.5 = (bf16[2,128,512]{2,1,0:T(8,128)(2,1)S(1)}, bf16[2,128,512]{2,1,0:T(8,128)(2,1)}, u32[]{:S(2)}, u32[]{:S(2)}) collective-permute-start(bf16[2,128,512]{2,1,0:T(8,128)(2,1)S(1)} %collective-permute-done.4), channel_id=1, source_target_pairs={{0,2},{1,15},{2,4},{3,1},{4,6},{5,3},{6,8},{7,5},{8,10},{9,7},{10,... | collective-permute-start | bytes 786440 | tf_op jit(solution)/shard_map/ppermute | solution.py:25
  50.0 0.0 copy-start.1
  50.1 3.8 %collective-permute-done.5 = bf16[2,128,512]{2,1,0:T(8,128)(2,1)} collective-permute-done((bf16[2,128,512]{2,1,0:T(8,128)(2,1)S(1)}, bf16[2,128,512]{2,1,0:T(8,128)(2,1)}, u32[]{:S(2)}, u32[]{:S(2)}) %collective-permute-start.5) | collective-permute-done | bytes 262176 | tf_op jit(solution)/shard_map/ppermute | solution.py:25
  53.8 4.8 %collective-permute-start.6 = (bf16[2,128,512]{2,1,0:T(8,128)(2,1)}, bf16[2,128,512]{2,1,0:T(8,128)(2,1)}, u32[]{:S(2)}, u32[]{:S(2)}) collective-permute-start(bf16[2,128,512]{2,1,0:T(8,128)(2,1)} %collective-permute-done.5), channel_id=1, source_target_pairs={{0,2},{1,15},{2,4},{3,1},{4,6},{5,3},{6,8},{7,5},{8,10},{9,7},{10,... | collective-permute-start | bytes 786440 | tf_op jit(solution)/shard_map/ppermute | solution.py:25
  58.6 1.0 fusion.29
  59.7 1.9 %collective-permute-start.7 = (bf16[3,128,512]{2,1,0:T(8,128)(2,1)S(1)}, bf16[3,128,512]{2,1,0:T(8,128)(2,1)S(1)}, u32[]{:S(2)}, u32[]{:S(2)}) collective-permute-start(bf16[3,128,512]{2,1,0:T(8,128)(2,1)S(1)} %pad_maximum_fusion), channel_id=1, source_target_pairs={{0,1},{1,0},{2,3},{3,2},{4,5},{5,4},{6,7},{7,6},{8,9},{9,8},{10,11... | collective-permute-start | bytes 1179656 | tf_op jit(solution)/shard_map/ppermute | solution.py:15
  61.6 0.0 copy-done.1
  61.6 0.8 fusion.15
  62.4 2.4 %collective-permute-start = (bf16[192,512]{1,0:T(8,128)(2,1)}, bf16[192,512]{1,0:T(8,128)(2,1)}, u32[]{:S(2)}, u32[]{:S(2)}) collective-permute-start(bf16[192,512]{1,0:T(8,128)(2,1)} %fusion.15), channel_id=1, source_target_pairs={{0,1},{1,0},{2,3},{3,2},{4,5},{5,4},{6,7},{7,6},{8,9},{9,8},{10,11... | collective-permute-start | bytes 589832 | tf_op jit(solution)/shard_map/ppermute | solution.py:15
  64.8 0.0 collective-permute-done.6
  64.8 0.9 slice_dynamic-update-slice_fusion.3
  65.8 0.0 collective-permute-done.7
  65.8 6.1 %all-to-all-done = bf16[128,24,128]{2,1,0:T(8,128)(2,1)S(1)} async-done(((bf16[128,24,128]{2,1,0:T(8,128)(2,1)}), bf16[128,24,128]{2,1,0:T(8,128)(2,1)S(1)}, u32[]{:S(2)}, u32[]{:S(2)}) %all-to-all-start) | async-done | bytes 786464 | tf_op jit(solution)/shard_map/all_to_all | solution.py:29
  71.9 0.3 reshape.62
  72.3 0.6 fusion.30
  72.8 0.1 slice_select_fusion
  72.9 3.0 %collective-permute-start.8 = (f32[192,512]{1,0:T(8,128)S(1)}, f32[192,512]{1,0:T(8,128)S(1)}, u32[]{:S(2)}, u32[]{:S(2)}) collective-permute-start(f32[192,512]{1,0:T(8,128)S(1)} %slice_select_fusion), channel_id=1, source_target_pairs={{0,1},{1,0},{2,3},{3,2},{4,5},{5,4},{6,7},{7,6},{8,9},{9,8},{10,11... | collective-permute-start | bytes 1179656 | tf_op jit(solution)/shard_map/ppermute | solution.py:15
  75.9 0.0 collective-permute-done
  75.9 1.1 broadcast_select_fusion.1
  77.0 0.2 collective-permute-done.8
  77.2 0.2 multiply_reduce_fusion
  77.5 0.8 all_to_all.14
  78.2 6.2 %all-to-all-start.2 = ((f32[64,1,3]{2,1,0:T(1,128)}), f32[64,1,3]{2,1,0:T(1,128)S(1)}, u32[]{:S(2)}, u32[]{:S(2)}) async-start(f32[64,1,3]{2,1,0:T(1,128)} %bitcast.12), calls=%async_computation.2 | async-start | bytes 65536 | tf_op jit(solution)/shard_map/all_to_all | solution.py:29
  84.5 1.7 %convolution_convert_fusion.1 = bf16[1024,512]{1,0:T(8,128)(2,1)} fusion(bf16[384,1024]{1,0:T(8,128)(2,1)S(1)} %reshape.62, bf16[192,512]{1,0:T(8,128)(2,1)S(1)} %get-tuple-element.12, bf16[192,512]{1,0:T(8,128)(2,1)S(1)} %get-tuple-element.11), kind=kOutput, calls=%fused_computation.2 | convolution fusion | flops 403963904 | bytes 2228224 | tf_op jit(solution)/shard_map/dot_general | solution.py:105
  86.2 9.1 %all-to-all-done.2 = f32[64,1,3]{2,1,0:T(1,128)S(1)} async-done(((f32[64,1,3]{2,1,0:T(1,128)}), f32[64,1,3]{2,1,0:T(1,128)S(1)}, u32[]{:S(2)}, u32[]{:S(2)}) %all-to-all-start.2) | async-done | bytes 800 | tf_op jit(solution)/shard_map/all_to_all | solution.py:29
  95.3 0.0 copy-start.3
  95.3 0.6 copy-done.3
  95.9 6.1 %all-to-all-start.1 = ((bf16[8,128,512]{2,1,0:T(8,128)(2,1)}), bf16[8,128,512]{2,1,0:T(8,128)(2,1)S(1)}, u32[]{:S(2)}, u32[]{:S(2)}) async-start(bf16[8,128,512]{2,1,0:T(8,128)(2,1)} %bitcast.30), calls=%async_computation.1 | async-start | bytes 2097152 | tf_op jit(solution)/shard_map/all_to_all | solution.py:29
  102.0 0.0 copy-start.5
  102.0 0.0 copy-start.6
  102.0 0.0 copy-start.7
  102.0 0.2 fusion.17
  102.2 0.8 pad_maximum_fusion.1
  103.0 0.5 broadcast.17
  103.5 0.0 copy-done.4
  103.5 0.7 reduce.3
  104.3 0.1 broadcast_in_dim.57
  104.4 0.0 copy-done.5
  104.4 0.0 copy-done.6
  104.4 0.0 copy-done.7
  104.4 0.2 select_reduce_fusion
  104.6 26.6 %all-to-all-done.1 = bf16[8,128,512]{2,1,0:T(8,128)(2,1)S(1)} async-done(((bf16[8,128,512]{2,1,0:T(8,128)(2,1)}), bf16[8,128,512]{2,1,0:T(8,128)(2,1)S(1)}, u32[]{:S(2)}, u32[]{:S(2)}) %all-to-all-start.1) | async-done | bytes 1048608 | tf_op jit(solution)/shard_map/all_to_all | solution.py:29
  131.2 0.1 convert_reduce_fusion
  131.3 2.4 %collective-permute-start.1 = (bf16[128,512]{1,0:T(8,128)(2,1)S(1)}, bf16[128,512]{1,0:T(8,128)(2,1)S(1)}, u32[]{:S(2)}, u32[]{:S(2)}) collective-permute-start(bf16[128,512]{1,0:T(8,128)(2,1)S(1)} %convert_element_type.62), channel_id=1, source_target_pairs={{0,512},{16,528},{32,544},{48,560},{64,576},{80,592},{96,608},{112... | collective-permute-start | bytes 393224 | tf_op jit(solution)/shard_map/ppermute | solution.py:15
  133.8 0.0 copy-done.8
  133.8 0.5 bitcast_divide_fusion
  134.3 8.1 %collective-permute-done.1 = bf16[128,512]{1,0:T(8,128)(2,1)S(1)} collective-permute-done((bf16[128,512]{1,0:T(8,128)(2,1)S(1)}, bf16[128,512]{1,0:T(8,128)(2,1)S(1)}, u32[]{:S(2)}, u32[]{:S(2)}) %collective-permute-start.1) | collective-permute-done | bytes 131104 | tf_op jit(solution)/shard_map/ppermute | solution.py:15
  142.3 0.7 add_bitcast_fusion
  (11 shorter events, 0.2 us)
Async XLA Ops:
  0.6 28.5 %copy-start = (bf16[128,2048]{1,0:T(8,128)(2,1)S(1)}, bf16[128,2048]{1,0:T(8,128)(2,1)}, u32[]{:S(2)}) copy-start(bf16[128,2048]{1,0:T(8,128)(2,1)} %param.7) | copy-start | bytes 1572868
  0.6 17.3 %collective-permute-start.2 = (bf16[128,512]{1,0:T(8,128)(2,1)}, bf16[128,512]{1,0:T(8,128)(2,1)S(1)}, u32[]{:S(2)}, u32[]{:S(2)}) collective-permute-start(bf16[128,512]{1,0:T(8,128)(2,1)} %bitcast.31), channel_id=1, source_target_pairs={{0,1},{1,0},{2,3},{3,2},{4,5},{5,4},{6,7},{7,6},{8,9},{9,8},{10,11... | collective-permute-start | bytes 393224 | tf_op jit(solution)/shard_map/ppermute | solution.py:15
  18.9 7.4 %collective-permute-start.3 = (bf16[2,128,512]{2,1,0:T(8,128)(2,1)S(1)}, bf16[2,128,512]{2,1,0:T(8,128)(2,1)S(1)}, u32[]{:S(2)}, u32[]{:S(2)}) collective-permute-start(bf16[2,128,512]{2,1,0:T(8,128)(2,1)S(1)} %pad_maximum_fusion.2), channel_id=1, source_target_pairs={{0,2},{1,15},{2,4},{3,1},{4,6},{5,3},{6,8},{7,5},{8,10},{9,7},{10,... | collective-permute-start | bytes 786440 | tf_op jit(solution)/shard_map/ppermute | solution.py:25
  26.3 20.0 %collective-permute-start.4 = (bf16[2,128,512]{2,1,0:T(8,128)(2,1)S(1)}, bf16[2,128,512]{2,1,0:T(8,128)(2,1)S(1)}, u32[]{:S(2)}, u32[]{:S(2)}) collective-permute-start(bf16[2,128,512]{2,1,0:T(8,128)(2,1)S(1)} %collective-permute-done.3), channel_id=1, source_target_pairs={{0,2},{1,15},{2,4},{3,1},{4,6},{5,3},{6,8},{7,5},{8,10},{9,7},{10,... | collective-permute-start | bytes 786440 | tf_op jit(solution)/shard_map/ppermute | solution.py:25
  31.9 14.4 %copy-start.2 = (bf16[1,128,512]{2,1,0:T(8,128)(2,1)S(1)}, bf16[1,128,512]{2,1,0:T(8,128)(2,1)}, u32[]{:S(2)}) copy-start(bf16[1,128,512]{2,1,0:T(8,128)(2,1)} %param.11) | copy-start | bytes 393220
  31.9 40.0 %all-to-all-start = ((bf16[128,24,128]{2,1,0:T(8,128)(2,1)}), bf16[128,24,128]{2,1,0:T(8,128)(2,1)S(1)}, u32[]{:S(2)}, u32[]{:S(2)}) async-start(bf16[128,24,128]{2,1,0:T(8,128)(2,1)} %bitcast.3), calls=%async_computation | async-start | bytes 1572864 | tf_op jit(solution)/shard_map/all_to_all | solution.py:29
  46.3 7.5 %collective-permute-start.5 = (bf16[2,128,512]{2,1,0:T(8,128)(2,1)S(1)}, bf16[2,128,512]{2,1,0:T(8,128)(2,1)}, u32[]{:S(2)}, u32[]{:S(2)}) collective-permute-start(bf16[2,128,512]{2,1,0:T(8,128)(2,1)S(1)} %collective-permute-done.4), channel_id=1, source_target_pairs={{0,2},{1,15},{2,4},{3,1},{4,6},{5,3},{6,8},{7,5},{8,10},{9,7},{10,... | collective-permute-start | bytes 786440 | tf_op jit(solution)/shard_map/ppermute | solution.py:25
  50.0 11.6 %copy-start.1 = (bf16[1,192,1024]{2,1,0:T(8,128)(2,1)S(1)}, bf16[1,192,1024]{2,1,0:T(8,128)(2,1)}, u32[]{:S(2)}) copy-start(bf16[1,192,1024]{2,1,0:T(8,128)(2,1)} %param.10) | copy-start | bytes 1179652
  53.8 11.0 %collective-permute-start.6 = (bf16[2,128,512]{2,1,0:T(8,128)(2,1)}, bf16[2,128,512]{2,1,0:T(8,128)(2,1)}, u32[]{:S(2)}, u32[]{:S(2)}) collective-permute-start(bf16[2,128,512]{2,1,0:T(8,128)(2,1)} %collective-permute-done.5), channel_id=1, source_target_pairs={{0,2},{1,15},{2,4},{3,1},{4,6},{5,3},{6,8},{7,5},{8,10},{9,7},{10,... | collective-permute-start | bytes 786440 | tf_op jit(solution)/shard_map/ppermute | solution.py:25
  59.7 6.1 %collective-permute-start.7 = (bf16[3,128,512]{2,1,0:T(8,128)(2,1)S(1)}, bf16[3,128,512]{2,1,0:T(8,128)(2,1)S(1)}, u32[]{:S(2)}, u32[]{:S(2)}) collective-permute-start(bf16[3,128,512]{2,1,0:T(8,128)(2,1)S(1)} %pad_maximum_fusion), channel_id=1, source_target_pairs={{0,1},{1,0},{2,3},{3,2},{4,5},{5,4},{6,7},{7,6},{8,9},{9,8},{10,11... | collective-permute-start | bytes 1179656 | tf_op jit(solution)/shard_map/ppermute | solution.py:15
  62.4 13.5 %collective-permute-start = (bf16[192,512]{1,0:T(8,128)(2,1)}, bf16[192,512]{1,0:T(8,128)(2,1)}, u32[]{:S(2)}, u32[]{:S(2)}) collective-permute-start(bf16[192,512]{1,0:T(8,128)(2,1)} %fusion.15), channel_id=1, source_target_pairs={{0,1},{1,0},{2,3},{3,2},{4,5},{5,4},{6,7},{7,6},{8,9},{9,8},{10,11... | collective-permute-start | bytes 589832 | tf_op jit(solution)/shard_map/ppermute | solution.py:15
  72.9 4.3 %collective-permute-start.8 = (f32[192,512]{1,0:T(8,128)S(1)}, f32[192,512]{1,0:T(8,128)S(1)}, u32[]{:S(2)}, u32[]{:S(2)}) collective-permute-start(f32[192,512]{1,0:T(8,128)S(1)} %slice_select_fusion), channel_id=1, source_target_pairs={{0,1},{1,0},{2,3},{3,2},{4,5},{5,4},{6,7},{7,6},{8,9},{9,8},{10,11... | collective-permute-start | bytes 1179656 | tf_op jit(solution)/shard_map/ppermute | solution.py:15
  78.2 17.1 %all-to-all-start.2 = ((f32[64,1,3]{2,1,0:T(1,128)}), f32[64,1,3]{2,1,0:T(1,128)S(1)}, u32[]{:S(2)}, u32[]{:S(2)}) async-start(f32[64,1,3]{2,1,0:T(1,128)} %bitcast.12), calls=%async_computation.2 | async-start | bytes 65536 | tf_op jit(solution)/shard_map/all_to_all | solution.py:29
  95.3 0.6 copy-start.3
  95.9 35.3 %all-to-all-start.1 = ((bf16[8,128,512]{2,1,0:T(8,128)(2,1)}), bf16[8,128,512]{2,1,0:T(8,128)(2,1)S(1)}, u32[]{:S(2)}, u32[]{:S(2)}) async-start(bf16[8,128,512]{2,1,0:T(8,128)(2,1)} %bitcast.30), calls=%async_computation.1 | async-start | bytes 2097152 | tf_op jit(solution)/shard_map/all_to_all | solution.py:29
  102.0 1.6 %copy-start.4 = (f32[64,1,3]{2,1,0:T(1,128)S(1)}, f32[64,1,3]{2,1,0:T(1,128)}, u32[]{:S(2)}) copy-start(f32[64,1,3]{2,1,0:T(1,128)} %copy-done.3) | copy-start | bytes 2308
  102.0 2.4 %copy-start.5 = (s32[192]{0:T(256)S(1)}, s32[192]{0:T(256)}, u32[]{:S(2)}) copy-start(s32[192]{0:T(256)} %constant.62) | copy-start | bytes 2308
  102.0 2.4 %copy-start.6 = (s32[192]{0:T(256)S(1)}, s32[192]{0:T(256)}, u32[]{:S(2)}) copy-start(s32[192]{0:T(256)} %constant.63) | copy-start | bytes 2308
  102.0 2.4 %copy-start.7 = (s32[128,1]{0,1:T(1,128)S(1)}, s32[128,1]{0,1:T(1,128)}, u32[]{:S(2)}) copy-start(s32[128,1]{0,1:T(1,128)} %param.9) | copy-start | bytes 1540
  103.0 30.7 %copy-start.8 = (bf16[128,1]{0,1:T(2,128)(2,1)S(1)}, bf16[128,1]{0,1:T(2,128)(2,1)}, u32[]{:S(2)}) copy-start(bf16[128,1]{0,1:T(2,128)(2,1)} %param.8) | copy-start | bytes 772
  131.3 11.0 %collective-permute-start.1 = (bf16[128,512]{1,0:T(8,128)(2,1)S(1)}, bf16[128,512]{1,0:T(8,128)(2,1)S(1)}, u32[]{:S(2)}, u32[]{:S(2)}) collective-permute-start(bf16[128,512]{1,0:T(8,128)(2,1)S(1)} %convert_element_type.62), channel_id=1, source_target_pairs={{0,512},{16,528},{32,544},{48,560},{64,576},{80,592},{96,608},{112... | collective-permute-start | bytes 393224 | tf_op jit(solution)/shard_map/ppermute | solution.py:15

commit v4 on v2

--- a/solution.py
+++ b/solution.py
@@ -1,5 +1,6 @@
 import jax
 import jax.numpy as jnp
+import numpy as np
 from jax import lax
 from jax.sharding import Mesh, PartitionSpec as P
 
@@ -54,8 +55,10 @@
         jnp.arange(tokens)[None, :] < jnp.arange(tokens)[:, None]
     )
     position = jnp.sum(same.astype(jnp.int32), axis=1)
-    target = ids * cap + position
-    place = target[:, None] == jnp.arange(rows, dtype=jnp.int32)[None, :]
+    row = np.arange(rows, dtype=np.int32)
+    place = (ids[:, None] == (row // cap)[None, :]) & (
+        position[:, None] == (row % cap)[None, :]
+    )
     probs = router_probs.astype(F32)
     spread = jnp.where(place, probs, 0.0).astype(BF)
     sent = lax.dot_general(
@@ -119,10 +122,12 @@
     grad_up = grad_act * silu
     grad_hidden = jnp.concatenate([grad_gate, grad_up], axis=1).astype(BF)[None]
     weighted = jnp.sum(grad_act * activation.astype(F32), axis=1)
-    back = exchange(weighted.reshape(slots, cap), "expert").reshape(rows)
-    grad_probs = (
-        jnp.sum(jnp.where(place, back[None, :], 0.0), axis=1, keepdims=True) / probs
-    )
+    sending = jnp.pad(weighted.reshape(slots, 1, cap), ((0, 0), (0, 0), (0, lanes - cap)))
+    back = exchange(sending, "expert").reshape(slots, lanes)
+    named = (ids[:, None] == jnp.arange(slots, dtype=jnp.int32)[None, :]).astype(F32)
+    picked = jnp.dot(named, back, precision=lax.Precision.HIGHEST)
+    lane = position[:, None] == jnp.arange(lanes, dtype=jnp.int32)[None, :]
+    grad_probs = jnp.sum(jnp.where(lane, picked, 0.0), axis=1, keepdims=True) / probs
     return (grad_down, grad_hidden, grad_probs)
 
 

time: 150 us -> 150 us (level)
  transfers between devices with their start and end apart: 12 -> 12, of which waited for: 7 -> 7; matrix products, arithmetic and copies ran while one was open for 9% -> 8% of each run, Pallas kernels for 0% -> 0%
where the time goes in v4:
time: 150 us; the launch traced here: 149 us
  starting transfers between devices  80.9 us (54%)
  waiting for transfers between devices  52.5 us (35%)
  other arithmetic  6.53 us (4%)
  local copies, waits for them, and re-layouts  4.44 us (3%)
  matrix products  3.8 us (3%)
    all_to_all x3, starting transfers between devices, exchange(): return lax.all_to_all(blocks, axis, split_axis=0, concat_axis=0, tiled=True)  37.8 us
    all_to_all x3, waiting for transfers between devices, exchange(): return lax.all_to_all(blocks, axis, split_axis=0, concat_axis=0, tiled=True)  37.3 us
    ppermute x5, starting transfers between devices, swap(): return lax.ppermute(block, axis, [(k, k ^ bit) for k in range(count)])  32.3 us
    ppermute x4, starting transfers between devices, fan(): return lax.ppermute(block, ('x', 'core'), route)  10.8 us
    ppermute x5, waiting for transfers between devices, swap(): return lax.ppermute(block, axis, [(k, k ^ bit) for k in range(count)])  8.28 us
    ppermute x4, waiting for transfers between devices, fan(): return lax.ppermute(block, ('x', 'core'), route)  6.96 us
  transfers between devices with their start and end apart: 12, of which 7 were waited for; matrix products, arithmetic and copies ran while one was open for 8% of the time, Pallas kernels for 0%

profile of v4, /device:TPU:1, one launch (start us, length us, event | category | flops | bytes accessed | tf_op | source)
XLA Modules:
  0.0 149.2 jit_solution(8557907797956371906)
XLA Ops:
  0.6 0.0 copy-start
  0.6 17.6 %collective-permute-start.2 = (bf16[128,512]{1,0:T(8,128)(2,1)}, bf16[128,512]{1,0:T(8,128)(2,1)S(1)}, u32[]{:S(2)}, u32[]{:S(2)}) collective-permute-start(bf16[128,512]{1,0:T(8,128)(2,1)} %bitcast.35), channel_id=1, source_target_pairs={{0,1},{1,0},{2,3},{3,2},{4,5},{5,4},{6,7},{7,6},{8,9},{9,8},{10,11... | collective-permute-start | bytes 393224 | tf_op jit(solution)/shard_map/ppermute | solution.py:15
  18.2 1.9 %collective-permute-start.6 = (bf16[128,512]{1,0:T(8,128)(2,1)}, bf16[128,512]{1,0:T(8,128)(2,1)}, u32[]{:S(2)}, u32[]{:S(2)}) collective-permute-start(bf16[128,512]{1,0:T(8,128)(2,1)} %bitcast.36), channel_id=1, source_target_pairs={{0,8},{1,9},{2,10},{3,11},{4,12},{5,13},{6,14},{7,15},{8,0},{9,1},... | collective-permute-start | bytes 393224 | tf_op jit(solution)/shard_map/ppermute | solution.py:25
  20.1 0.9 convert_reduce_fusion.1
  21.0 0.0 collective-permute-done.2
  21.1 0.9 pad_maximum_fusion.2
  22.0 1.9 %collective-permute-start.3 = (bf16[2,128,512]{2,1,0:T(8,128)(2,1)S(1)}, bf16[2,128,512]{2,1,0:T(8,128)(2,1)S(1)}, u32[]{:S(2)}, u32[]{:S(2)}) collective-permute-start(bf16[2,128,512]{2,1,0:T(8,128)(2,1)S(1)} %pad_maximum_fusion.2), channel_id=1, source_target_pairs={{0,2},{1,15},{2,4},{3,1},{4,6},{5,3},{6,8},{7,5},{8,10},{9,7},{10,... | collective-permute-start | bytes 786440 | tf_op jit(solution)/shard_map/ppermute | solution.py:25
  23.9 0.0 copy-done
  23.9 1.2 convolution_convert_fusion
  25.1 0.6 reshape.60
  25.7 1.0 copy.13
  26.7 0.0 copy-start.2
  26.7 21.3 %all-to-all-start = ((bf16[128,24,128]{2,1,0:T(8,128)(2,1)}), bf16[128,24,128]{2,1,0:T(8,128)(2,1)S(1)}, u32[]{:S(2)}, u32[]{:S(2)}) async-start(bf16[128,24,128]{2,1,0:T(8,128)(2,1)} %bitcast.3), calls=%async_computation | async-start | bytes 1572864 | tf_op jit(solution)/shard_map/all_to_all | solution.py:29
  48.0 1.9 %collective-permute-start.4 = (bf16[2,128,512]{2,1,0:T(8,128)(2,1)S(1)}, bf16[2,128,512]{2,1,0:T(8,128)(2,1)S(1)}, u32[]{:S(2)}, u32[]{:S(2)}) collective-permute-start(bf16[2,128,512]{2,1,0:T(8,128)(2,1)S(1)} %pad_maximum_fusion.2), channel_id=1, source_target_pairs={{0,4},{1,13},{2,6},{3,15},{4,8},{5,1},{6,10},{7,3},{8,12},{9,5},{1... | collective-permute-start | bytes 786440 | tf_op jit(solution)/shard_map/ppermute | solution.py:25
  49.9 0.1 broadcast_in_dim.52
  50.0 0.0 copy-done.2
  50.1 5.0 %collective-permute-start.5 = (bf16[2,128,512]{2,1,0:T(8,128)(2,1)S(1)}, bf16[2,128,512]{2,1,0:T(8,128)(2,1)S(1)}, u32[]{:S(2)}, u32[]{:S(2)}) collective-permute-start(bf16[2,128,512]{2,1,0:T(8,128)(2,1)S(1)} %pad_maximum_fusion.2), channel_id=1, source_target_pairs={{0,6},{1,11},{2,8},{3,13},{4,10},{5,15},{6,12},{7,1},{8,14},{9,3},... | collective-permute-start | bytes 786440 | tf_op jit(solution)/shard_map/ppermute | solution.py:25
  55.1 0.0 collective-permute-done.3
  55.1 0.0 copy-start.1
  55.1 4.1 %collective-permute-done.4 = bf16[2,128,512]{2,1,0:T(8,128)(2,1)S(1)} collective-permute-done((bf16[2,128,512]{2,1,0:T(8,128)(2,1)S(1)}, bf16[2,128,512]{2,1,0:T(8,128)(2,1)S(1)}, u32[]{:S(2)}, u32[]{:S(2)}) %collective-permute-start.4) | collective-permute-done | bytes 262176 | tf_op jit(solution)/shard_map/ppermute | solution.py:25
  59.2 2.9 %collective-permute-done.5 = bf16[2,128,512]{2,1,0:T(8,128)(2,1)S(1)} collective-permute-done((bf16[2,128,512]{2,1,0:T(8,128)(2,1)S(1)}, bf16[2,128,512]{2,1,0:T(8,128)(2,1)S(1)}, u32[]{:S(2)}, u32[]{:S(2)}) %collective-permute-start.5) | collective-permute-done | bytes 262176 | tf_op jit(solution)/shard_map/ppermute | solution.py:25
  62.2 7.4 %collective-permute-start.7 = (bf16[3,128,512]{2,1,0:T(8,128)(2,1)S(1)}, bf16[3,128,512]{2,1,0:T(8,128)(2,1)S(1)}, u32[]{:S(2)}, u32[]{:S(2)}) collective-permute-start(bf16[3,128,512]{2,1,0:T(8,128)(2,1)S(1)} %pad_maximum_fusion), channel_id=1, source_target_pairs={{0,1},{1,0},{2,3},{3,2},{4,5},{5,4},{6,7},{7,6},{8,9},{9,8},{10,11... | collective-permute-start | bytes 1179656 | tf_op jit(solution)/shard_map/ppermute | solution.py:15
  69.6 0.0 copy-done.1
  69.6 0.8 fusion.16
  70.4 1.9 %collective-permute-start = (bf16[192,512]{1,0:T(8,128)(2,1)}, bf16[192,512]{1,0:T(8,128)(2,1)}, u32[]{:S(2)}, u32[]{:S(2)}) collective-permute-start(bf16[192,512]{1,0:T(8,128)(2,1)} %fusion.16), channel_id=1, source_target_pairs={{0,1},{1,0},{2,3},{3,2},{4,5},{5,4},{6,7},{7,6},{8,9},{9,8},{10,11... | collective-permute-start | bytes 589832 | tf_op jit(solution)/shard_map/ppermute | solution.py:15
  72.4 0.0 collective-permute-done.6
  72.4 0.9 bitcast_dynamic-update-slice_fusion
  73.3 0.0 collective-permute-done.7
  73.4 0.4 all-to-all-done
  73.7 0.3 reshape.62
  74.1 0.6 fusion.32
  74.6 0.1 slice_select_fusion
  74.7 3.0 %collective-permute-start.8 = (f32[192,512]{1,0:T(8,128)S(1)}, f32[192,512]{1,0:T(8,128)S(1)}, u32[]{:S(2)}, u32[]{:S(2)}) collective-permute-start(f32[192,512]{1,0:T(8,128)S(1)} %slice_select_fusion), channel_id=1, source_target_pairs={{0,1},{1,0},{2,3},{3,2},{4,5},{5,4},{6,7},{7,6},{8,9},{9,8},{10,11... | collective-permute-start | bytes 1179656 | tf_op jit(solution)/shard_map/ppermute | solution.py:15
  77.7 0.0 collective-permute-done
  77.7 1.1 broadcast_select_fusion.1
  78.8 0.2 collective-permute-done.8
  79.1 0.2 multiply_reduce_fusion
  79.3 0.1 reshape.65
  79.4 0.6 pad.4
  80.1 11.0 %all-to-all-start.2 = ((f32[64,1,128]{2,1,0:T(1,128)}), f32[64,1,128]{2,1,0:T(1,128)S(1)}, u32[]{:S(2)}, u32[]{:S(2)}) async-start(f32[64,1,128]{2,1,0:T(1,128)} %bitcast.13), calls=%async_computation.2 | async-start | bytes 65536 | tf_op jit(solution)/shard_map/all_to_all | solution.py:29
  91.1 1.7 %convolution_convert_fusion.1 = bf16[1024,512]{1,0:T(8,128)(2,1)} fusion(bf16[384,1024]{1,0:T(8,128)(2,1)S(1)} %reshape.62, bf16[192,512]{1,0:T(8,128)(2,1)S(1)} %get-tuple-element.12, bf16[192,512]{1,0:T(8,128)(2,1)S(1)} %get-tuple-element.11), kind=kOutput, calls=%fused_computation.2 | convolution fusion | flops 403963904 | bytes 2228224 | tf_op jit(solution)/shard_map/dot_general | solution.py:104
  92.8 9.1 %all-to-all-done.2 = f32[64,1,128]{2,1,0:T(1,128)S(1)} async-done(((f32[64,1,128]{2,1,0:T(1,128)}), f32[64,1,128]{2,1,0:T(1,128)S(1)}, u32[]{:S(2)}, u32[]{:S(2)}) %all-to-all-start.2) | async-done | bytes 32800 | tf_op jit(solution)/shard_map/all_to_all | solution.py:29
  101.9 0.0 copy-start.3
  101.9 0.6 copy-done.3
  102.5 5.5 %all-to-all-start.1 = ((bf16[8,128,512]{2,1,0:T(8,128)(2,1)}), bf16[8,128,512]{2,1,0:T(8,128)(2,1)S(1)}, u32[]{:S(2)}, u32[]{:S(2)}) async-start(bf16[8,128,512]{2,1,0:T(8,128)(2,1)} %bitcast.34), calls=%async_computation.1 | async-start | bytes 2097152 | tf_op jit(solution)/shard_map/all_to_all | solution.py:29
  108.0 0.0 copy-start.4
  108.0 0.0 copy-start.5
  108.0 0.2 fusion.18
  108.3 0.8 pad_maximum_fusion.1
  109.1 0.0 copy-start.6
  109.1 0.0 copy-done.4
  109.1 0.0 copy-done.5
  109.1 0.3 fusion
  109.4 27.9 %all-to-all-done.1 = bf16[8,128,512]{2,1,0:T(8,128)(2,1)S(1)} async-done(((bf16[8,128,512]{2,1,0:T(8,128)(2,1)}), bf16[8,128,512]{2,1,0:T(8,128)(2,1)S(1)}, u32[]{:S(2)}, u32[]{:S(2)}) %all-to-all-start.1) | async-done | bytes 1048608 | tf_op jit(solution)/shard_map/all_to_all | solution.py:29
  137.2 0.1 convert_reduce_fusion
  137.4 2.4 %collective-permute-start.1 = (bf16[128,512]{1,0:T(8,128)(2,1)S(1)}, bf16[128,512]{1,0:T(8,128)(2,1)S(1)}, u32[]{:S(2)}, u32[]{:S(2)}) collective-permute-start(bf16[128,512]{1,0:T(8,128)(2,1)S(1)} %convert_element_type.65), channel_id=1, source_target_pairs={{0,512},{16,528},{32,544},{48,560},{64,576},{80,592},{96,608},{112... | collective-permute-start | bytes 393224 | tf_op jit(solution)/shard_map/ppermute | solution.py:15
  139.8 0.0 copy-done.6
  139.8 0.5 bitcast_divide_fusion
  140.4 8.1 %collective-permute-done.1 = bf16[128,512]{1,0:T(8,128)(2,1)S(1)} collective-permute-done((bf16[128,512]{1,0:T(8,128)(2,1)S(1)}, bf16[128,512]{1,0:T(8,128)(2,1)S(1)}, u32[]{:S(2)}, u32[]{:S(2)}) %collective-permute-start.1) | collective-permute-done | bytes 131104 | tf_op jit(solution)/shard_map/ppermute | solution.py:15
  148.4 0.7 add_bitcast_fusion
  (9 shorter events, 0.2 us)
Async XLA Ops:
  0.6 23.3 %copy-start = (bf16[128,2048]{1,0:T(8,128)(2,1)S(1)}, bf16[128,2048]{1,0:T(8,128)(2,1)}, u32[]{:S(2)}) copy-start(bf16[128,2048]{1,0:T(8,128)(2,1)} %param.7) | copy-start | bytes 1572868
  0.6 20.4 %collective-permute-start.2 = (bf16[128,512]{1,0:T(8,128)(2,1)}, bf16[128,512]{1,0:T(8,128)(2,1)S(1)}, u32[]{:S(2)}, u32[]{:S(2)}) collective-permute-start(bf16[128,512]{1,0:T(8,128)(2,1)} %bitcast.35), channel_id=1, source_target_pairs={{0,1},{1,0},{2,3},{3,2},{4,5},{5,4},{6,7},{7,6},{8,9},{9,8},{10,11... | collective-permute-start | bytes 393224 | tf_op jit(solution)/shard_map/ppermute | solution.py:15
  18.2 54.2 %collective-permute-start.6 = (bf16[128,512]{1,0:T(8,128)(2,1)}, bf16[128,512]{1,0:T(8,128)(2,1)}, u32[]{:S(2)}, u32[]{:S(2)}) collective-permute-start(bf16[128,512]{1,0:T(8,128)(2,1)} %bitcast.36), channel_id=1, source_target_pairs={{0,8},{1,9},{2,10},{3,11},{4,12},{5,13},{6,14},{7,15},{8,0},{9,1},... | collective-permute-start | bytes 393224 | tf_op jit(solution)/shard_map/ppermute | solution.py:25
  22.0 33.1 %collective-permute-start.3 = (bf16[2,128,512]{2,1,0:T(8,128)(2,1)S(1)}, bf16[2,128,512]{2,1,0:T(8,128)(2,1)S(1)}, u32[]{:S(2)}, u32[]{:S(2)}) collective-permute-start(bf16[2,128,512]{2,1,0:T(8,128)(2,1)S(1)} %pad_maximum_fusion.2), channel_id=1, source_target_pairs={{0,2},{1,15},{2,4},{3,1},{4,6},{5,3},{6,8},{7,5},{8,10},{9,7},{10,... | collective-permute-start | bytes 786440 | tf_op jit(solution)/shard_map/ppermute | solution.py:25
  26.7 23.3 %copy-start.2 = (bf16[1,128,512]{2,1,0:T(8,128)(2,1)S(1)}, bf16[1,128,512]{2,1,0:T(8,128)(2,1)}, u32[]{:S(2)}) copy-start(bf16[1,128,512]{2,1,0:T(8,128)(2,1)} %param.11) | copy-start | bytes 393220
  26.7 47.0 %all-to-all-start = ((bf16[128,24,128]{2,1,0:T(8,128)(2,1)}), bf16[128,24,128]{2,1,0:T(8,128)(2,1)S(1)}, u32[]{:S(2)}, u32[]{:S(2)}) async-start(bf16[128,24,128]{2,1,0:T(8,128)(2,1)} %bitcast.3), calls=%async_computation | async-start | bytes 1572864 | tf_op jit(solution)/shard_map/all_to_all | solution.py:29
  48.0 11.2 %collective-permute-start.4 = (bf16[2,128,512]{2,1,0:T(8,128)(2,1)S(1)}, bf16[2,128,512]{2,1,0:T(8,128)(2,1)S(1)}, u32[]{:S(2)}, u32[]{:S(2)}) collective-permute-start(bf16[2,128,512]{2,1,0:T(8,128)(2,1)S(1)} %pad_maximum_fusion.2), channel_id=1, source_target_pairs={{0,4},{1,13},{2,6},{3,15},{4,8},{5,1},{6,10},{7,3},{8,12},{9,5},{1... | collective-permute-start | bytes 786440 | tf_op jit(solution)/shard_map/ppermute | solution.py:25
  50.1 12.1 %collective-permute-start.5 = (bf16[2,128,512]{2,1,0:T(8,128)(2,1)S(1)}, bf16[2,128,512]{2,1,0:T(8,128)(2,1)S(1)}, u32[]{:S(2)}, u32[]{:S(2)}) collective-permute-start(bf16[2,128,512]{2,1,0:T(8,128)(2,1)S(1)} %pad_maximum_fusion.2), channel_id=1, source_target_pairs={{0,6},{1,11},{2,8},{3,13},{4,10},{5,15},{6,12},{7,1},{8,14},{9,3},... | collective-permute-start | bytes 786440 | tf_op jit(solution)/shard_map/ppermute | solution.py:25
  55.1 14.5 %copy-start.1 = (bf16[1,192,1024]{2,1,0:T(8,128)(2,1)S(1)}, bf16[1,192,1024]{2,1,0:T(8,128)(2,1)}, u32[]{:S(2)}) copy-start(bf16[1,192,1024]{2,1,0:T(8,128)(2,1)} %param.10) | copy-start | bytes 1179652
  62.2 11.1 %collective-permute-start.7 = (bf16[3,128,512]{2,1,0:T(8,128)(2,1)S(1)}, bf16[3,128,512]{2,1,0:T(8,128)(2,1)S(1)}, u32[]{:S(2)}, u32[]{:S(2)}) collective-permute-start(bf16[3,128,512]{2,1,0:T(8,128)(2,1)S(1)} %pad_maximum_fusion), channel_id=1, source_target_pairs={{0,1},{1,0},{2,3},{3,2},{4,5},{5,4},{6,7},{7,6},{8,9},{9,8},{10,11... | collective-permute-start | bytes 1179656 | tf_op jit(solution)/shard_map/ppermute | solution.py:15
  70.4 7.3 %collective-permute-start = (bf16[192,512]{1,0:T(8,128)(2,1)}, bf16[192,512]{1,0:T(8,128)(2,1)}, u32[]{:S(2)}, u32[]{:S(2)}) collective-permute-start(bf16[192,512]{1,0:T(8,128)(2,1)} %fusion.16), channel_id=1, source_target_pairs={{0,1},{1,0},{2,3},{3,2},{4,5},{5,4},{6,7},{7,6},{8,9},{9,8},{10,11... | collective-permute-start | bytes 589832 | tf_op jit(solution)/shard_map/ppermute | solution.py:15
  74.7 4.3 %collective-permute-start.8 = (f32[192,512]{1,0:T(8,128)S(1)}, f32[192,512]{1,0:T(8,128)S(1)}, u32[]{:S(2)}, u32[]{:S(2)}) collective-permute-start(f32[192,512]{1,0:T(8,128)S(1)} %slice_select_fusion), channel_id=1, source_target_pairs={{0,1},{1,0},{2,3},{3,2},{4,5},{5,4},{6,7},{7,6},{8,9},{9,8},{10,11... | collective-permute-start | bytes 1179656 | tf_op jit(solution)/shard_map/ppermute | solution.py:15
  80.1 21.8 %all-to-all-start.2 = ((f32[64,1,128]{2,1,0:T(1,128)}), f32[64,1,128]{2,1,0:T(1,128)S(1)}, u32[]{:S(2)}, u32[]{:S(2)}) async-start(f32[64,1,128]{2,1,0:T(1,128)} %bitcast.13), calls=%async_computation.2 | async-start | bytes 65536 | tf_op jit(solution)/shard_map/all_to_all | solution.py:29
  101.9 0.6 copy-start.3
  102.5 34.7 %all-to-all-start.1 = ((bf16[8,128,512]{2,1,0:T(8,128)(2,1)}), bf16[8,128,512]{2,1,0:T(8,128)(2,1)S(1)}, u32[]{:S(2)}, u32[]{:S(2)}) async-start(bf16[8,128,512]{2,1,0:T(8,128)(2,1)} %bitcast.34), calls=%async_computation.1 | async-start | bytes 2097152 | tf_op jit(solution)/shard_map/all_to_all | solution.py:29
  108.0 1.0 copy-start.4
  108.0 1.0 copy-start.5
  109.1 30.8 %copy-start.6 = (bf16[128,1]{0,1:T(2,128)(2,1)S(1)}, bf16[128,1]{0,1:T(2,128)(2,1)}, u32[]{:S(2)}) copy-start(bf16[128,1]{0,1:T(2,128)(2,1)} %param.8) | copy-start | bytes 772
  137.4 11.0 %collective-permute-start.1 = (bf16[128,512]{1,0:T(8,128)(2,1)S(1)}, bf16[128,512]{1,0:T(8,128)(2,1)S(1)}, u32[]{:S(2)}, u32[]{:S(2)}) collective-permute-start(bf16[128,512]{1,0:T(8,128)(2,1)S(1)} %convert_element_type.65), channel_id=1, source_target_pairs={{0,512},{16,528},{32,544},{48,560},{64,576},{80,592},{96,608},{112... | collective-permute-start | bytes 393224 | tf_op jit(solution)/shard_map/ppermute | solution.py:15

commit v5 on v4

--- a/solution.py
+++ b/solution.py
@@ -124,10 +124,11 @@
     weighted = jnp.sum(grad_act * activation.astype(F32), axis=1)
     sending = jnp.pad(weighted.reshape(slots, 1, cap), ((0, 0), (0, 0), (0, lanes - cap)))
     back = exchange(sending, "expert").reshape(slots, lanes)
-    named = (ids[:, None] == jnp.arange(slots, dtype=jnp.int32)[None, :]).astype(F32)
+    slot_row = jnp.arange(slots, dtype=jnp.int32)[None, :]
+    named = jnp.where(ids[:, None] == slot_row, 1.0 / probs, 0.0)
     picked = jnp.dot(named, back, precision=lax.Precision.HIGHEST)
     lane = position[:, None] == jnp.arange(lanes, dtype=jnp.int32)[None, :]
-    grad_probs = jnp.sum(jnp.where(lane, picked, 0.0), axis=1, keepdims=True) / probs
+    grad_probs = jnp.sum(jnp.where(lane, picked, 0.0), axis=1, keepdims=True)
     return (grad_down, grad_hidden, grad_probs)
 
 

time: 150 us -> 139 us (0.927)
  waiting for transfers between devices: 52.5 us -> 33.6 us
  starting transfers between devices: 80.9 us -> 85.7 us
  matrix products: 3.8 us -> 6.66 us
    all_to_all x3, waiting for transfers between devices: 37.3 us -> 25.5 us  [exchange(): return lax.all_to_all(blocks, axis, split_axis=0, concat_axis=0, tiled=True)]
    ppermute x5, waiting for transfers between devices: 8.28 us -> 1.39 us  [swap(): return lax.ppermute(block, axis, [(k, k ^ bit) for k in range(count)])]
    ppermute x5, starting transfers between devices: 32.3 us -> 39.1 us  [swap(): return lax.ppermute(block, axis, [(k, k ^ bit) for k in range(count)])]
    all_to_all x3, starting transfers between devices: 37.8 us -> 36 us  [exchange(): return lax.all_to_all(blocks, axis, split_axis=0, concat_axis=0, tiled=True)]
  transfers between devices with their start and end apart: 12 -> 12, of which waited for: 7 -> 5; matrix products, arithmetic and copies ran while one was open for 8% -> 9% of each run, Pallas kernels for 0% -> 0%
where the time goes in v5:
time: 139 us; the launch traced here: 138 us
  starting transfers between devices  85.7 us (62%)
  waiting for transfers between devices  33.6 us (24%)
  matrix products  6.66 us (5%)
  other arithmetic  6.48 us (5%)
  local copies, waits for them, and re-layouts  4.83 us (3%)
    ppermute x5, starting transfers between devices, swap(): return lax.ppermute(block, axis, [(k, k ^ bit) for k in range(count)])  39.1 us
    all_to_all x3, starting transfers between devices, exchange(): return lax.all_to_all(blocks, axis, split_axis=0, concat_axis=0, tiled=True)  36 us
    all_to_all x3, waiting for transfers between devices, exchange(): return lax.all_to_all(blocks, axis, split_axis=0, concat_axis=0, tiled=True)  25.5 us
    ppermute x4, starting transfers between devices, fan(): return lax.ppermute(block, ('x', 'core'), route)  10.6 us
    ppermute x4, waiting for transfers between devices, fan(): return lax.ppermute(block, ('x', 'core'), route)  6.71 us
    dot_general x1, matrix products, on_device(): lax.dot_general(scaled, both, (((0,), (0,)), ((), ())), preferred_element...  2.89 us
  transfers between devices with their start and end apart: 12, of which 5 were waited for; matrix products, arithmetic and copies ran while one was open for 9% of the time, Pallas kernels for 0%

profile of v5, /device:TPU:1, one launch (start us, length us, event | category | flops | bytes accessed | tf_op | source)
XLA Modules:
  0.0 138.3 jit_solution(14541026771100334857)
XLA Ops:
  0.6 0.0 copy-start
  0.6 17.6 %collective-permute-start.2 = (bf16[128,512]{1,0:T(8,128)(2,1)}, bf16[128,512]{1,0:T(8,128)(2,1)S(1)}, u32[]{:S(2)}, u32[]{:S(2)}) collective-permute-start(bf16[128,512]{1,0:T(8,128)(2,1)} %bitcast.36), channel_id=1, source_target_pairs={{0,1},{1,0},{2,3},{3,2},{4,5},{5,4},{6,7},{7,6},{8,9},{9,8},{10,11... | collective-permute-start | bytes 393224 | tf_op jit(solution)/shard_map/ppermute | solution.py:15
  18.2 1.9 %collective-permute-start.6 = (bf16[128,512]{1,0:T(8,128)(2,1)}, bf16[128,512]{1,0:T(8,128)(2,1)S(1)}, u32[]{:S(2)}, u32[]{:S(2)}) collective-permute-start(bf16[128,512]{1,0:T(8,128)(2,1)} %bitcast.37), channel_id=1, source_target_pairs={{0,8},{1,9},{2,10},{3,11},{4,12},{5,13},{6,14},{7,15},{8,0},{9,1},... | collective-permute-start | bytes 393224 | tf_op jit(solution)/shard_map/ppermute | solution.py:25
  20.1 0.9 convert_reduce_fusion.1
  21.0 0.0 copy-done
  21.1 1.2 convolution_convert_fusion
  22.3 0.6 reshape.60
  22.8 1.0 copy.13
  23.8 0.0 copy-start.2
  23.8 0.0 copy-start.1
  23.9 17.9 %all-to-all-start = ((bf16[128,24,128]{2,1,0:T(8,128)(2,1)}), bf16[128,24,128]{2,1,0:T(8,128)(2,1)S(1)}, u32[]{:S(2)}, u32[]{:S(2)}) async-start(bf16[128,24,128]{2,1,0:T(8,128)(2,1)} %bitcast.3), calls=%async_computation | async-start | bytes 1572864 | tf_op jit(solution)/shard_map/all_to_all | solution.py:29
  41.7 0.0 collective-permute-done.2
  41.7 0.0 copy-done.2
  41.7 0.7 pad_maximum_fusion.2
  42.5 2.2 %collective-permute-start.3 = (bf16[2,128,512]{2,1,0:T(8,128)(2,1)}, bf16[2,128,512]{2,1,0:T(8,128)(2,1)S(1)}, u32[]{:S(2)}, u32[]{:S(2)}) collective-permute-start(bf16[2,128,512]{2,1,0:T(8,128)(2,1)} %pad_maximum_fusion.2), channel_id=1, source_target_pairs={{0,2},{1,15},{2,4},{3,1},{4,6},{5,3},{6,8},{7,5},{8,10},{9,7},{10,... | collective-permute-start | bytes 786440 | tf_op jit(solution)/shard_map/ppermute | solution.py:25
  44.6 0.0 copy-done.1
  44.7 0.8 fusion.16
  45.5 5.6 %collective-permute-start = (bf16[192,512]{1,0:T(8,128)(2,1)}, bf16[192,512]{1,0:T(8,128)(2,1)}, u32[]{:S(2)}, u32[]{:S(2)}) collective-permute-start(bf16[192,512]{1,0:T(8,128)(2,1)} %fusion.16), channel_id=1, source_target_pairs={{0,1},{1,0},{2,3},{3,2},{4,5},{5,4},{6,7},{7,6},{8,9},{9,8},{10,11... | collective-permute-start | bytes 589832 | tf_op jit(solution)/shard_map/ppermute | solution.py:15
  51.1 1.9 %collective-permute-start.4 = (bf16[2,128,512]{2,1,0:T(8,128)(2,1)}, bf16[2,128,512]{2,1,0:T(8,128)(2,1)}, u32[]{:S(2)}, u32[]{:S(2)}) collective-permute-start(bf16[2,128,512]{2,1,0:T(8,128)(2,1)} %pad_maximum_fusion.2), channel_id=1, source_target_pairs={{0,4},{1,13},{2,6},{3,15},{4,8},{5,1},{6,10},{7,3},{8,12},{9,5},{1... | collective-permute-start | bytes 786440 | tf_op jit(solution)/shard_map/ppermute | solution.py:25
  53.0 0.1 broadcast_in_dim.66
  53.2 4.6 %collective-permute-start.5 = (bf16[2,128,512]{2,1,0:T(8,128)(2,1)}, bf16[2,128,512]{2,1,0:T(8,128)(2,1)S(1)}, u32[]{:S(2)}, u32[]{:S(2)}) collective-permute-start(bf16[2,128,512]{2,1,0:T(8,128)(2,1)} %pad_maximum_fusion.2), channel_id=1, source_target_pairs={{0,6},{1,11},{2,8},{3,13},{4,10},{5,15},{6,12},{7,1},{8,14},{9,3},... | collective-permute-start | bytes 786440 | tf_op jit(solution)/shard_map/ppermute | solution.py:25
  57.8 0.0 collective-permute-done.3
  57.8 4.6 %collective-permute-done.4 = bf16[2,128,512]{2,1,0:T(8,128)(2,1)} collective-permute-done((bf16[2,128,512]{2,1,0:T(8,128)(2,1)}, bf16[2,128,512]{2,1,0:T(8,128)(2,1)}, u32[]{:S(2)}, u32[]{:S(2)}) %collective-permute-start.4) | collective-permute-done | bytes 262176 | tf_op jit(solution)/shard_map/ppermute | solution.py:25
  62.5 1.0 fusion.34
  63.5 2.1 %collective-permute-done.5 = bf16[2,128,512]{2,1,0:T(8,128)(2,1)S(1)} collective-permute-done((bf16[2,128,512]{2,1,0:T(8,128)(2,1)}, bf16[2,128,512]{2,1,0:T(8,128)(2,1)S(1)}, u32[]{:S(2)}, u32[]{:S(2)}) %collective-permute-start.5) | collective-permute-done | bytes 262176 | tf_op jit(solution)/shard_map/ppermute | solution.py:25
  65.6 6.8 %collective-permute-start.7 = (bf16[3,128,512]{2,1,0:T(8,128)(2,1)S(1)}, bf16[3,128,512]{2,1,0:T(8,128)(2,1)S(1)}, u32[]{:S(2)}, u32[]{:S(2)}) collective-permute-start(bf16[3,128,512]{2,1,0:T(8,128)(2,1)S(1)} %pad_maximum_fusion), channel_id=1, source_target_pairs={{0,1},{1,0},{2,3},{3,2},{4,5},{5,4},{6,7},{7,6},{8,9},{9,8},{10,11... | collective-permute-start | bytes 1179656 | tf_op jit(solution)/shard_map/ppermute | solution.py:15
  72.5 0.0 collective-permute-done
  72.5 1.8 %broadcast_select_fusion.1 = (bf16[192,512]{1,0:T(8,128)(2,1)S(1)}, bf16[192,512]{1,0:T(8,128)(2,1)}) fusion(bf16[192,512]{1,0:T(8,128)(2,1)} %collective-permute-done, pred[]{:T(512)S(6)} %eq.84, bf16[192,1024]{1,0:T(8,128)(2,1)S(1)} %bitcast.31), kind=kLoop, calls=%fused_computation.38 | loop fusion | flops 983040 | bytes 983041 | tf_op jit(solution)/shard_map/jit(_where)/select_n | solution.py:98
  74.2 0.0 collective-permute-done.6
  74.3 0.0 collective-permute-done.7
  74.3 0.0 all-to-all-done
  74.3 1.3 reshape.62
  75.6 2.9 %convolution_convert_fusion.1 = bf16[1024,512]{1,0:T(8,128)(2,1)} fusion(bf16[384,1024]{1,0:T(8,128)(2,1)} %reshape.62, bf16[192,512]{1,0:T(8,128)(2,1)} %get-tuple-element.12, bf16[192,512]{1,0:T(8,128)(2,1)S(1)} %get-tuple-element.11), kind=kOutput, calls=%fused_computation.2 | convolution fusion | flops 403963904 | bytes 2228224 | tf_op jit(solution)/shard_map/dot_general | solution.py:104
  78.5 5.5 %all-to-all-start.1 = ((bf16[8,128,512]{2,1,0:T(8,128)(2,1)}), bf16[8,128,512]{2,1,0:T(8,128)(2,1)S(1)}, u32[]{:S(2)}, u32[]{:S(2)}) async-start(bf16[8,128,512]{2,1,0:T(8,128)(2,1)} %bitcast.35), calls=%async_computation.1 | async-start | bytes 2097152 | tf_op jit(solution)/shard_map/all_to_all | solution.py:29
  84.0 1.7 %fusion.36 = f32[384,512]{1,0:T(8,128)S(1)} fusion(bf16[384,1024]{1,0:T(8,128)(2,1)} %reshape.62, bf16[1024,512]{1,0:T(8,128)(2,1)S(1)} %bitcast.34), kind=kOutput, calls=%fused_computation.72 | convolution fusion | flops 402653184 | bytes 2621440 | tf_op jit(solution)/shard_map/dot_general | solution.py:113
  85.8 0.0 copy-start.3
  85.8 0.1 slice_select_fusion
  85.8 2.2 %collective-permute-start.8 = (f32[192,512]{1,0:T(8,128)S(1)}, f32[192,512]{1,0:T(8,128)S(1)}, u32[]{:S(2)}, u32[]{:S(2)}) collective-permute-start(f32[192,512]{1,0:T(8,128)S(1)} %slice_select_fusion), channel_id=1, source_target_pairs={{0,1},{1,0},{2,3},{3,2},{4,5},{5,4},{6,7},{7,6},{8,9},{9,8},{10,11... | collective-permute-start | bytes 1179656 | tf_op jit(solution)/shard_map/ppermute | solution.py:15
  88.0 0.0 copy-done.3
  88.1 1.4 %collective-permute-done.8 = f32[192,512]{1,0:T(8,128)S(1)} collective-permute-done((f32[192,512]{1,0:T(8,128)S(1)}, f32[192,512]{1,0:T(8,128)S(1)}, u32[]{:S(2)}, u32[]{:S(2)}) %collective-permute-start.8) | collective-permute-done | bytes 393248 | tf_op jit(solution)/shard_map/ppermute | solution.py:15
  89.4 0.2 multiply_reduce_fusion
  89.7 0.1 reshape.65
  89.8 0.6 pad.4
  90.5 0.2 fusion.18
  90.7 22.6 %all-to-all-done.1 = bf16[8,128,512]{2,1,0:T(8,128)(2,1)S(1)} async-done(((bf16[8,128,512]{2,1,0:T(8,128)(2,1)}), bf16[8,128,512]{2,1,0:T(8,128)(2,1)S(1)}, u32[]{:S(2)}, u32[]{:S(2)}) %all-to-all-start.1) | async-done | bytes 1048608 | tf_op jit(solution)/shard_map/all_to_all | solution.py:29
  113.3 12.6 %all-to-all-start.2 = ((f32[64,1,128]{2,1,0:T(1,128)}), f32[64,1,128]{2,1,0:T(1,128)S(1)}, u32[]{:S(2)}, u32[]{:S(2)}) async-start(f32[64,1,128]{2,1,0:T(1,128)} %bitcast.14), calls=%async_computation.2 | async-start | bytes 65536 | tf_op jit(solution)/shard_map/all_to_all | solution.py:29
  125.9 0.0 copy-start.4
  125.9 0.1 convert_reduce_fusion
  126.1 6.9 %collective-permute-start.1 = (bf16[128,512]{1,0:T(8,128)(2,1)S(1)}, bf16[128,512]{1,0:T(8,128)(2,1)S(1)}, u32[]{:S(2)}, u32[]{:S(2)}) collective-permute-start(bf16[128,512]{1,0:T(8,128)(2,1)S(1)} %convert_element_type.64), channel_id=1, source_target_pairs={{0,512},{16,528},{32,544},{48,560},{64,576},{80,592},{96,608},{112... | collective-permute-start | bytes 393224 | tf_op jit(solution)/shard_map/ppermute | solution.py:15
  133.0 0.8 pad_maximum_fusion.1
  133.8 2.9 %all-to-all-done.2 = f32[64,1,128]{2,1,0:T(1,128)S(1)} async-done(((f32[64,1,128]{2,1,0:T(1,128)}), f32[64,1,128]{2,1,0:T(1,128)S(1)}, u32[]{:S(2)}, u32[]{:S(2)}) %all-to-all-start.2) | async-done | bytes 32800 | tf_op jit(solution)/shard_map/all_to_all | solution.py:29
  136.7 0.0 copy-done.4
  136.7 0.9 fusion
  137.6 0.0 collective-permute-done.1
  137.6 0.7 add_bitcast_fusion
  (10 shorter events, 0.2 us)
Async XLA Ops:
  0.6 20.4 %copy-start = (bf16[128,2048]{1,0:T(8,128)(2,1)S(1)}, bf16[128,2048]{1,0:T(8,128)(2,1)}, u32[]{:S(2)}) copy-start(bf16[128,2048]{1,0:T(8,128)(2,1)} %param.7) | copy-start | bytes 1572868
  0.6 41.1 %collective-permute-start.2 = (bf16[128,512]{1,0:T(8,128)(2,1)}, bf16[128,512]{1,0:T(8,128)(2,1)S(1)}, u32[]{:S(2)}, u32[]{:S(2)}) collective-permute-start(bf16[128,512]{1,0:T(8,128)(2,1)} %bitcast.36), channel_id=1, source_target_pairs={{0,1},{1,0},{2,3},{3,2},{4,5},{5,4},{6,7},{7,6},{8,9},{9,8},{10,11... | collective-permute-start | bytes 393224 | tf_op jit(solution)/shard_map/ppermute | solution.py:15
  18.2 56.0 %collective-permute-start.6 = (bf16[128,512]{1,0:T(8,128)(2,1)}, bf16[128,512]{1,0:T(8,128)(2,1)S(1)}, u32[]{:S(2)}, u32[]{:S(2)}) collective-permute-start(bf16[128,512]{1,0:T(8,128)(2,1)} %bitcast.37), channel_id=1, source_target_pairs={{0,8},{1,9},{2,10},{3,11},{4,12},{5,13},{6,14},{7,15},{8,0},{9,1},... | collective-permute-start | bytes 393224 | tf_op jit(solution)/shard_map/ppermute | solution.py:25
  23.8 17.9 %copy-start.2 = (bf16[1,128,512]{2,1,0:T(8,128)(2,1)S(1)}, bf16[1,128,512]{2,1,0:T(8,128)(2,1)}, u32[]{:S(2)}) copy-start(bf16[1,128,512]{2,1,0:T(8,128)(2,1)} %param.11) | copy-start | bytes 393220
  23.8 20.8 %copy-start.1 = (bf16[1,192,1024]{2,1,0:T(8,128)(2,1)S(1)}, bf16[1,192,1024]{2,1,0:T(8,128)(2,1)}, u32[]{:S(2)}) copy-start(bf16[1,192,1024]{2,1,0:T(8,128)(2,1)} %param.10) | copy-start | bytes 1179652
  23.9 50.5 %all-to-all-start = ((bf16[128,24,128]{2,1,0:T(8,128)(2,1)}), bf16[128,24,128]{2,1,0:T(8,128)(2,1)S(1)}, u32[]{:S(2)}, u32[]{:S(2)}) async-start(bf16[128,24,128]{2,1,0:T(8,128)(2,1)} %bitcast.3), calls=%async_computation | async-start | bytes 1572864 | tf_op jit(solution)/shard_map/all_to_all | solution.py:29
  42.5 15.3 %collective-permute-start.3 = (bf16[2,128,512]{2,1,0:T(8,128)(2,1)}, bf16[2,128,512]{2,1,0:T(8,128)(2,1)S(1)}, u32[]{:S(2)}, u32[]{:S(2)}) collective-permute-start(bf16[2,128,512]{2,1,0:T(8,128)(2,1)} %pad_maximum_fusion.2), channel_id=1, source_target_pairs={{0,2},{1,15},{2,4},{3,1},{4,6},{5,3},{6,8},{7,5},{8,10},{9,7},{10,... | collective-permute-start | bytes 786440 | tf_op jit(solution)/shard_map/ppermute | solution.py:25
  45.5 27.0 %collective-permute-start = (bf16[192,512]{1,0:T(8,128)(2,1)}, bf16[192,512]{1,0:T(8,128)(2,1)}, u32[]{:S(2)}, u32[]{:S(2)}) collective-permute-start(bf16[192,512]{1,0:T(8,128)(2,1)} %fusion.16), channel_id=1, source_target_pairs={{0,1},{1,0},{2,3},{3,2},{4,5},{5,4},{6,7},{7,6},{8,9},{9,8},{10,11... | collective-permute-start | bytes 589832 | tf_op jit(solution)/shard_map/ppermute | solution.py:15
  51.1 11.4 %collective-permute-start.4 = (bf16[2,128,512]{2,1,0:T(8,128)(2,1)}, bf16[2,128,512]{2,1,0:T(8,128)(2,1)}, u32[]{:S(2)}, u32[]{:S(2)}) collective-permute-start(bf16[2,128,512]{2,1,0:T(8,128)(2,1)} %pad_maximum_fusion.2), channel_id=1, source_target_pairs={{0,4},{1,13},{2,6},{3,15},{4,8},{5,1},{6,10},{7,3},{8,12},{9,5},{1... | collective-permute-start | bytes 786440 | tf_op jit(solution)/shard_map/ppermute | solution.py:25
  53.2 12.4 %collective-permute-start.5 = (bf16[2,128,512]{2,1,0:T(8,128)(2,1)}, bf16[2,128,512]{2,1,0:T(8,128)(2,1)S(1)}, u32[]{:S(2)}, u32[]{:S(2)}) collective-permute-start(bf16[2,128,512]{2,1,0:T(8,128)(2,1)} %pad_maximum_fusion.2), channel_id=1, source_target_pairs={{0,6},{1,11},{2,8},{3,13},{4,10},{5,15},{6,12},{7,1},{8,14},{9,3},... | collective-permute-start | bytes 786440 | tf_op jit(solution)/shard_map/ppermute | solution.py:25
  65.6 8.7 %collective-permute-start.7 = (bf16[3,128,512]{2,1,0:T(8,128)(2,1)S(1)}, bf16[3,128,512]{2,1,0:T(8,128)(2,1)S(1)}, u32[]{:S(2)}, u32[]{:S(2)}) collective-permute-start(bf16[3,128,512]{2,1,0:T(8,128)(2,1)S(1)} %pad_maximum_fusion), channel_id=1, source_target_pairs={{0,1},{1,0},{2,3},{3,2},{4,5},{5,4},{6,7},{7,6},{8,9},{9,8},{10,11... | collective-permute-start | bytes 1179656 | tf_op jit(solution)/shard_map/ppermute | solution.py:15
  78.5 34.8 %all-to-all-start.1 = ((bf16[8,128,512]{2,1,0:T(8,128)(2,1)}), bf16[8,128,512]{2,1,0:T(8,128)(2,1)S(1)}, u32[]{:S(2)}, u32[]{:S(2)}) async-start(bf16[8,128,512]{2,1,0:T(8,128)(2,1)} %bitcast.35), calls=%async_computation.1 | async-start | bytes 2097152 | tf_op jit(solution)/shard_map/all_to_all | solution.py:29
  85.8 2.3 %copy-start.3 = (bf16[128,1]{0,1:T(2,128)(2,1)S(1)}, bf16[128,1]{0,1:T(2,128)(2,1)}, u32[]{:S(2)}) copy-start(bf16[128,1]{0,1:T(2,128)(2,1)} %param.8) | copy-start | bytes 772
  85.8 3.6 %collective-permute-start.8 = (f32[192,512]{1,0:T(8,128)S(1)}, f32[192,512]{1,0:T(8,128)S(1)}, u32[]{:S(2)}, u32[]{:S(2)}) collective-permute-start(f32[192,512]{1,0:T(8,128)S(1)} %slice_select_fusion), channel_id=1, source_target_pairs={{0,1},{1,0},{2,3},{3,2},{4,5},{5,4},{6,7},{7,6},{8,9},{9,8},{10,11... | collective-permute-start | bytes 1179656 | tf_op jit(solution)/shard_map/ppermute | solution.py:15
  113.3 23.4 %all-to-all-start.2 = ((f32[64,1,128]{2,1,0:T(1,128)}), f32[64,1,128]{2,1,0:T(1,128)S(1)}, u32[]{:S(2)}, u32[]{:S(2)}) async-start(f32[64,1,128]{2,1,0:T(1,128)} %bitcast.14), calls=%async_computation.2 | async-start | bytes 65536 | tf_op jit(solution)/shard_map/all_to_all | solution.py:29
  125.9 10.8 %copy-start.4 = (s32[128,1]{0,1:T(1,128)S(1)}, s32[128,1]{0,1:T(1,128)}, u32[]{:S(2)}) copy-start(s32[128,1]{0,1:T(1,128)} %param.9) | copy-start | bytes 1540
  126.1 11.5 %collective-permute-start.1 = (bf16[128,512]{1,0:T(8,128)(2,1)S(1)}, bf16[128,512]{1,0:T(8,128)(2,1)S(1)}, u32[]{:S(2)}, u32[]{:S(2)}) collective-permute-start(bf16[128,512]{1,0:T(8,128)(2,1)S(1)} %convert_element_type.64), channel_id=1, source_target_pairs={{0,512},{16,528},{32,544},{48,560},{64,576},{80,592},{96,608},{112... | collective-permute-start | bytes 393224 | tf_op jit(solution)/shard_map/ppermute | solution.py:15
